TPU v7x, 32 devices: a whole 2x2x4 slice. The times are simulated.
32 devices in a mesh: scen: 4 (over y, core), node: 8 (over z, x).
Axes of the slice: x: 2, y: 2, z: 4, core: 2. Of those that a mesh axis runs over, the one named last changes fastest.
Arguments:
- factors: bfloat16 [8, 4, 1024, 1024], P('node', 'scen'), may hold values from -0.1875 to 0.1875
- couple: bfloat16 [8, 4, 1024, 512], P('node', 'scen'), may hold values from -0.1875 to 0.1875
- leaf_rhs: bfloat16 [8, 4, 2, 1024], P('node', 'scen'), may hold values from -6 to 6
- node_diag: float32 [8, 512, 512], P('node', 'scen'), as said below
- node_rhs: float32 [8, 2, 512], P('node', None, 'scen'), may hold values from -6 to 6
- link_root: float32 [8, 512, 512], P('node', 'scen'), may hold values from -1.5 to 1.5
- root_diag: float32 [512, 512], replicated, as said below
- root_rhs: float32 [2, 512], replicated, may hold values from -6 to 6
Outputs:
- leaf_solution: float32 [8, 4, 2, 1024], P('node', 'scen')
- node_solution: float32 [8, 2, 512], P('node', None, 'scen')
- root_solution: float32 [2, 512], replicated
Inputs may be any that keep to these rules, and one draw needn't show every extreme that they name: `node_diag`: symmetric positive definite. `root_diag`: symmetric positive definite.
All inputs are finite; a program needn't handle non-finite values.
Results may differ from a plain program's by a relative error of at most 0.0036.
Values sent between devices are 32-bit elements; how exact they have to be, the bound alone decides.
No kernel may reach another device: no remote copies, remote signals or barrier semaphores. Data moves between devices by JAX's collectives and lax.ppermute only.
A program may use at most 64 MiB of HBM per device.

v0:
```python
import jax
import jax.numpy as jnp
from jax import lax
from jax.sharding import PartitionSpec as P

HIGH = lax.Precision.HIGHEST


def local(factors, couple, leaf_rhs, node_diag, node_rhs, link_root, root_diag, root_rhs):
    factor = factors[0, 0]
    coupling = couple[0, 0]
    rights = leaf_rhs[0, 0]
    share = node_diag.shape[1]
    offset = lax.axis_index("scen") * share
    link_full = lax.all_gather(link_root[0], "scen", axis=0, tiled=True)
    reduced = lax.dot_general(
        factor, coupling, (((0,), (0,)), ((), ())), preferred_element_type=jnp.float32
    ).astype(jnp.bfloat16)
    projected = jnp.dot(rights, factor, preferred_element_type=jnp.float32)
    schur_term = lax.dot_general(
        reduced, reduced, (((0,), (0,)), ((), ())), preferred_element_type=jnp.float32
    )
    rhs_term = jnp.dot(projected.astype(jnp.bfloat16), reduced, preferred_element_type=jnp.float32)
    band = lax.dynamic_slice_in_dim(schur_term, offset, share, 0) + node_diag[0]
    schur_term = lax.dynamic_update_slice_in_dim(schur_term, band, offset, 0)
    strip = lax.dynamic_slice_in_dim(rhs_term, offset, share, 1) + node_rhs[0]
    rhs_term = lax.dynamic_update_slice_in_dim(rhs_term, strip, offset, 1)
    node_matrix, node_vector = lax.psum((schur_term, rhs_term), "scen")
    lower = jnp.linalg.cholesky(node_matrix)
    solved_rhs = jax.scipy.linalg.cho_solve((lower, True), node_vector.T)
    solved_link = jax.scipy.linalg.cho_solve((lower, True), link_full)
    root_part = jnp.dot(link_full.T, solved_link, precision=HIGH)
    root_vec = jnp.dot(link_full.T, solved_rhs, precision=HIGH)
    root_matrix, root_vector = lax.psum((root_part, root_vec), "node")
    root_lower = jnp.linalg.cholesky(root_matrix + root_diag)
    root_sol = jax.scipy.linalg.cho_solve((root_lower, True), root_vector - root_rhs.T)
    shifted = node_vector.T - jnp.dot(link_full, root_sol, precision=HIGH)
    node_sol = jax.scipy.linalg.cho_solve((lower, True), shifted)
    update = jnp.dot(reduced, node_sol.astype(jnp.bfloat16), preferred_element_type=jnp.float32)
    difference = (update.T - projected).astype(jnp.bfloat16)
    leaf_sol = lax.dot_general(
        difference, factor, (((1,), (1,)), ((), ())), preferred_element_type=jnp.float32
    )
    node_part = lax.dynamic_slice_in_dim(node_sol.T, offset, share, 1)
    return (leaf_sol[None, None], node_part[None], root_sol.T)


def solution(mesh):
    placed = (
        P("node", "scen", None, None),
        P("node", "scen", None, None),
        P("node", "scen", None, None),
        P("node", "scen", None),
        P("node", None, "scen"),
        P("node", "scen", None),
        P(),
        P(),
    )
    return jax.shard_map(
        local,
        mesh=mesh,
        in_specs=placed,
        out_specs=(P("node", "scen", None, None), P("node", None, "scen"), P()),
        check_vma=False,
    )
```

profile of v0, /device:TPU:0, one launch (start us, length us, event | category | flops | bytes accessed | tf_op | source)
XLA Modules:
  0.0 495.0 jit_solution(5571907004051996018)
XLA Ops:
  17.8 8.6 %psum.29 = f32[512,2]{0,1:T(2,128)S(1)} all-reduce(f32[512,2]{0,1:T(2,128)S(1)} %bitcast.230), channel_id=1, replica_groups=mesh['scen'=4,'node'=8] {'scen'}, use_global_device_ids=true, to_apply=%region_9.11 | all-reduce | flops 1024 | bytes 8192 | tf_op jit(solution)/shard_map/psum | solution.py:28
  29.0 26.0 %all-reduce.4.cloned.1.call-done = f32[512,512]{0,1:T(8,128)} async-done(((f32[512,512]{0,1:T(8,128)}), f32[512,512]{0,1:T(8,128)}) %all-reduce.4.cloned.1.call-update) | async-done | bytes 1048592 | tf_op jit(solution)/shard_map/psum | solution.py:28
  60.1 11.7 %cholesky.286 = f32[128,128]{1,0:T(8,128)S(1)} custom-call(f32[128,128]{1,0:T(8,128)S(1)} %cholesky.426), custom_call_target="Cholesky" | custom-call | tf_op jit(solution)/shard_map/jit(cholesky)/cholesky | solution.py:29
  72.0 9.8 %custom-call.38 = f32[1,128,128]{1,2,0:T(8,128)S(1)} custom-call(f32[1,128,128]{2,1,0:T(8,128)S(1)} %get-tuple-element.75), custom_call_target="InvertDiagBlocksLowerTriangular" | custom-call | tf_op jit(solution)/shard_map/jit(cholesky)/cholesky | solution.py:29
  85.0 11.7 %cholesky.305 = f32[128,128]{1,0:T(8,128)S(1)} custom-call(f32[128,128]{1,0:T(8,128)S(1)} %cholesky.430), custom_call_target="Cholesky" | custom-call | tf_op jit(solution)/shard_map/jit(cholesky)/cholesky | solution.py:29
  97.3 10.3 %custom-call.39 = f32[1,128,128]{1,2,0:T(8,128)S(1)} custom-call(f32[1,128,128]{2,1,0:T(8,128)S(1)} %get-tuple-element.72), custom_call_target="InvertDiagBlocksLowerTriangular" | custom-call | tf_op jit(solution)/shard_map/jit(cholesky)/cholesky | solution.py:29
  110.1 11.7 %cholesky.326 = f32[128,128]{1,0:T(8,128)S(1)} custom-call(f32[128,128]{1,0:T(8,128)S(1)} %cholesky.435), custom_call_target="Cholesky" | custom-call | tf_op jit(solution)/shard_map/jit(cholesky)/cholesky | solution.py:29
  122.4 9.8 %custom-call.40 = f32[1,128,128]{1,2,0:T(8,128)S(1)} custom-call(f32[1,128,128]{2,1,0:T(8,128)S(1)} %get-tuple-element.69), custom_call_target="InvertDiagBlocksLowerTriangular" | custom-call | tf_op jit(solution)/shard_map/jit(cholesky)/cholesky | solution.py:29
  133.6 11.9 %cholesky.343 = f32[128,128]{1,0:T(8,128)S(1)} custom-call(f32[128,128]{1,0:T(8,128)S(1)} %convolution_subtract_fusion.11), custom_call_target="Cholesky" | custom-call | tf_op jit(solution)/shard_map/jit(cholesky)/cholesky | solution.py:29
  153.4 8.5 %while.8 = (s32[]{:T(128)}, f32[512,512]{1,0:T(8,128)S(1)}, s32[4,2]{0,1:T(2,128)S(1)}, f32[4,128,128]{2,1,0:T(8,128)S(1)}, s32[]{:T(128)}) while((s32[]{:T(128)}, f32[512,512]{1,0:T(8,128)S(1)}, s32[4,2]{0,1:T(2,128)S(1)}, f32[4,128,128]{2,1,0:T(8,128)S(1)}, s32[]{:T(128)}) %tuple.61), condition=%wide.while_cond.clone.1, body=%wide.while_body.clone.1.sunk | while | flops 2 | bytes 131189 | solution.py:38
  162.5 40.2 %custom-call.46 = f32[4,128,128]{1,2,0:T(8,128)S(1)} custom-call(f32[4,128,128]{2,1,0:T(8,128)} %copy-done.12), custom_call_target="InvertDiagBlocksLowerTriangular" | custom-call | tf_op jit(solution)/shard_map/jit(_cho_solve)/triangular_solve | solution.py:38
  214.5 2.9 convolution_bitcast_fusion
  219.6 21.9 %psum.31 = f32[512,2]{0,1:T(2,128)S(1)} all-reduce(f32[512,2]{0,1:T(2,128)S(1)} %convolution_bitcast_fusion.2), channel_id=1, replica_groups=mesh['scen'=4,'node'=8] {'node'}, use_global_device_ids=true, to_apply=%region_11.14 | all-reduce | flops 1024 | bytes 8192 | tf_op jit(solution)/shard_map/psum | solution.py:34
  242.1 54.3 %all-reduce.6.cloned.1.call-done = f32[512,512]{0,1:T(8,128)} async-done(((f32[512,512]{0,1:T(8,128)}), f32[512,512]{0,1:T(8,128)}) %all-reduce.6.cloned.1.call-update) | async-done | bytes 1048592 | tf_op jit(solution)/shard_map/psum | solution.py:34
  304.4 11.7 %cholesky.358 = f32[128,128]{1,0:T(8,128)S(1)} custom-call(f32[128,128]{1,0:T(8,128)S(1)} %cholesky.439), custom_call_target="Cholesky" | custom-call | tf_op jit(solution)/shard_map/jit(cholesky)/cholesky | solution.py:35
  317.8 9.8 %custom-call.41 = f32[1,128,128]{1,2,0:T(8,128)S(1)} custom-call(f32[1,128,128]{2,1,0:T(8,128)S(1)} %get-tuple-element.65), custom_call_target="InvertDiagBlocksLowerTriangular" | custom-call | tf_op jit(solution)/shard_map/jit(cholesky)/cholesky | solution.py:35
  331.5 11.7 %cholesky.377 = f32[128,128]{1,0:T(8,128)S(1)} custom-call(f32[128,128]{1,0:T(8,128)S(1)} %cholesky.443), custom_call_target="Cholesky" | custom-call | tf_op jit(solution)/shard_map/jit(cholesky)/cholesky | solution.py:35
  344.4 10.2 %custom-call.42 = f32[1,128,128]{1,2,0:T(8,128)S(1)} custom-call(f32[1,128,128]{2,1,0:T(8,128)S(1)} %get-tuple-element.62), custom_call_target="InvertDiagBlocksLowerTriangular" | custom-call | tf_op jit(solution)/shard_map/jit(cholesky)/cholesky | solution.py:35
  358.5 13.2 %cholesky.398 = f32[128,128]{1,0:T(8,128)} custom-call(f32[128,128]{1,0:T(8,128)} %cholesky.448), custom_call_target="Cholesky" | custom-call | tf_op jit(solution)/shard_map/jit(cholesky)/cholesky | solution.py:35
  373.7 11.3 %custom-call.43 = f32[1,128,128]{1,2,0:T(8,128)} custom-call(f32[1,128,128]{2,1,0:T(8,128)} %get-tuple-element.59), custom_call_target="InvertDiagBlocksLowerTriangular" | custom-call | tf_op jit(solution)/shard_map/jit(cholesky)/cholesky | solution.py:35
  388.1 11.9 %cholesky.415 = f32[128,128]{1,0:T(8,128)S(1)} custom-call(f32[128,128]{1,0:T(8,128)S(1)} %convolution_subtract_fusion.10), custom_call_target="Cholesky" | custom-call | tf_op jit(solution)/shard_map/jit(cholesky)/cholesky | solution.py:35
  410.7 13.6 %while.7 = (s32[]{:T(128)}, f32[512,512]{1,0:T(8,128)}, s32[4,2]{0,1:T(2,128)S(1)}, f32[4,128,128]{2,1,0:T(8,128)}, s32[]{:T(128)}) while((s32[]{:T(128)}, f32[512,512]{1,0:T(8,128)}, s32[4,2]{0,1:T(2,128)S(1)}, f32[4,128,128]{2,1,0:T(8,128)}, s32[]{:T(128)}) %tuple.73), condition=%wide.while_cond.clone, body=%wide.while_body.clone.sunk | while | flops 2 | bytes 132205 | solution.py:36
  411.3 2.8 bitcast_dynamic-update-slice_fusion.4
  424.2 40.7 %custom-call.45 = f32[4,128,128]{1,2,0:T(8,128)} custom-call(f32[4,128,128]{2,1,0:T(8,128)} %get-tuple-element.34), custom_call_target="InvertDiagBlocksLowerTriangular" | custom-call | tf_op jit(solution)/shard_map/jit(_cho_solve)/triangular_solve | solution.py:36
  (181 shorter events, 121.4 us)
Async XLA Ops:
  7.2 1.6 copy-start
  7.2 47.8 %all-reduce.4.cloned.1.call-start = ((), (), s32[]{:S(2)}) async-start(), calls=%async_computation | async-start | bytes 2097152 | tf_op jit(solution)/shard_map/psum | solution.py:28
  11.3 6.3 %copy-start.7 = (bf16[1024,512]{1,0:T(8,128)(2,1)}, bf16[1024,512]{1,0:T(8,128)(2,1)S(1)}, u32[]{:S(2)}) copy-start(bf16[1024,512]{1,0:T(8,128)(2,1)S(1)} %fusion.6) | copy-start | bytes 3145732
  13.0 4.2 copy-start.14
  15.8 2.0 copy-start.16
  15.9 189.3 %all-gather.3.cloned.1.call-start = ((), (), s32[]{:S(2)}) async-start(), calls=%async_computation.2 | async-start | bytes 1310720 | tf_op jit(solution)/shard_map/all_gather | solution.py:15
  16.6 279.8 %all-reduce.6.cloned.1.call-start = ((), (), s32[]{:S(2)}) async-start(), calls=%async_computation.1 | async-start | bytes 2097152 | tf_op jit(solution)/shard_map/psum | solution.py:34
  55.0 2.6 copy-start.6
  59.1 1.0 copy-start.8
  84.4 0.7 copy-start.10
  145.5 5.8 %copy-start.5 = (f32[512,512]{1,0:T(8,128)}, f32[512,512]{1,0:T(8,128)S(1)}, u32[]{:S(2)}) copy-start(f32[512,512]{1,0:T(8,128)S(1)} %get-tuple-element.67) | copy-start | bytes 3145732
  161.9 0.7 copy-start.12
  162.5 42.6 %copy-start.2 = (f32[512,512]{1,0:T(8,128)}, f32[512,512]{1,0:T(8,128)S(1)}, u32[]{:S(2)}) copy-start(f32[512,512]{1,0:T(8,128)S(1)} %get-tuple-element.174) | copy-start | bytes 3145732
  205.2 3.3 copy-start.1
  205.2 5.1 %copy-start.3 = (f32[512,512]{1,0:T(8,128)S(1)}, f32[512,512]{1,0:T(8,128)}, u32[]{:S(2)}) copy-start(f32[512,512]{1,0:T(8,128)} %copy-done.2) | copy-start | bytes 3145732
  214.4 27.0 %copy-start.15 = (f32[2,512]{1,0:T(2,128)S(1)}, f32[2,512]{1,0:T(2,128)}, u32[]{:S(2)}) copy-start(f32[2,512]{1,0:T(2,128)} %param.18) | copy-start | bytes 12292
  303.4 1.0 copy-start.9
  330.8 0.7 copy-start.11
  400.0 65.0 %copy-start.13 = (f32[512,2]{0,1:T(2,128)S(1)}, f32[512,2]{0,1:T(2,128)}, u32[]{:S(2)}) copy-start(f32[512,2]{0,1:T(2,128)} %bitcast_subtract_fusion) | copy-start | bytes 12292
  465.0 16.4 %copy-start.4 = (f32[512,512]{1,0:T(8,128)S(1)}, f32[512,512]{1,0:T(8,128)}, u32[]{:S(2)}) copy-start(f32[512,512]{1,0:T(8,128)} %copy-done.2) | copy-start | bytes 3145732
Sparse Core Ops, SparseCore 0:
  16.0 38.9 all-reduce.3
  56.6 17.2 all-gather.2
  217.5 78.8 all-reduce.5
where the time goes:
time: 500 us; the launch traced here: 495 us
  other arithmetic  264 us (53%)
  waiting for transfers between devices  81.1 us (16%)
  matrix products  59.5 us (12%)
  local copies, waits for them, and re-layouts  40.2 us (8%)
  blocking collectives  30.5 us (6%)
  between operations  19.4 us (4%)
    another operation x15, other arithmetic, local(): root_lower = jnp.linalg.cholesky(root_matrix + root_diag)  88.6 us
    another operation x14, other arithmetic, local(): lower = jnp.linalg.cholesky(node_matrix)  81.5 us
    psum x1, waiting for transfers between devices, local(): root_matrix, root_vector = lax.psum((root_part, root_vec), 'node')  54.3 us
    another operation x2, other arithmetic, local(): jax.scipy.linalg.cho_solve((root_lower, True), root_vector - root_rhs.T)  43.1 us
    another operation x4, other arithmetic, local(): node_sol = jax.scipy.linalg.cho_solve((lower, True), shifted)  42.1 us
    psum x1, waiting for transfers between devices, local(): node_matrix, node_vector = lax.psum((schur_term, rhs_term), 'scen')  26 us
    psum x1, blocking collectives, local(): root_matrix, root_vector = lax.psum((root_part, root_vec), 'node')  21.9 us
    another operation x14, matrix products, local(): jax.scipy.linalg.cho_solve((root_lower, True), root_vector - root_rhs.T)  15.2 us
  transfers between devices with their start and end apart: 3, of which 2 were waited for; matrix products, arithmetic and copies ran while one was open for 31% of the time, Pallas kernels for 0%

commit v1 on v0

v1 whole, which is shorter than its diff:
```python
import jax
import jax.numpy as jnp
from jax import lax
from jax.experimental import pallas as pl
from jax.experimental.pallas import tpu as pltpu
from jax.sharding import PartitionSpec as P

F32, BF16 = jnp.float32, jnp.bfloat16
NN, NT, TN = ((1,), (0,)), ((1,), (1,)), ((0,), (0,))
ROWS = 8
PARTS = 4
NEAR = 2


def dot(a, b, dims):
    return lax.dot_general(a, b, (dims, ((), ())), preferred_element_type=F32)


def thirds(x):
    high = x.astype(BF16)
    rest = x - high.astype(F32)
    mid = rest.astype(BF16)
    return high, mid, (rest - mid.astype(F32)).astype(BF16)


def exact(a, b, dims):
    (ah, am, al), (bh, bm, bl) = thirds(a), thirds(b)
    left = jnp.concatenate([ah, ah, am, am, ah, al], dims[0][0])
    right = jnp.concatenate([bh, bm, bh, bm, bl, bh], dims[1][0])
    return dot(left, right, dims)


def rank_update(u):
    high = u.astype(BF16).astype(F32)
    rest = u - high
    mid = rest.astype(BF16).astype(F32)
    low = rest - mid
    left = jnp.concatenate([high, high, mid, mid, high, low], 0).astype(BF16)
    right = jnp.concatenate([high, mid, high, mid, low, high], 0).astype(BF16)
    return dot(left, right, TN)


def from_lane(x, i):
    return jnp.broadcast_to(x[:, i : i + 1], x.shape)


def from_row(x, i):
    return jnp.take_along_axis(x, jnp.full(x.shape, i, jnp.int32), axis=0)


def invert_factor(rows, store, hook):
    shape = rows[0].shape
    lane = lax.broadcasted_iota(jnp.int32, shape, 1)
    sub = lax.broadcasted_iota(jnp.int32, shape, 0)
    groups = len(rows)
    for k in range(groups):
        first = ROWS * k
        inside = (lane >= first) & (lane < first + ROWS)
        cols = [from_lane(rows[k], first + i) for i in range(ROWS)]
        piv = {(m, i): from_row(cols[i], m) for i in range(ROWS) for m in range(i, ROWS)}
        panel = jnp.where(inside, jnp.where(lane - first == sub, 1.0, 0.0), rows[k])
        line = [jnp.broadcast_to(panel[i : i + 1, :], shape) for i in range(ROWS)]
        near = range(k + 1, min(k + 1 + NEAR, groups))
        mult = {g: [from_lane(rows[g], first + i) for i in range(ROWS)] for g in near}
        kept = {g: jnp.where(inside, 0.0, rows[g]) for g in near}
        for i in range(ROWS):
            inverse = 1.0 / piv[i, i]
            ratio = {m: piv[m, i] * inverse for m in range(i + 1, ROWS)}
            for m in range(i + 1, ROWS):
                for p in range(i + 1, m + 1):
                    piv[m, p] = piv[m, p] - ratio[m] * piv[p, i]
            for m in range(i + 1, ROWS):
                line[m] = line[m] - ratio[m] * line[i]
            for g in near:
                for p in range(i + 1, ROWS):
                    mult[g][p] = mult[g][p] - mult[g][i] * ratio[p]
                kept[g] = kept[g] - (mult[g][i] * inverse) * line[i]
        for g in near:
            rows[g] = kept[g]
        out = line[0] * lax.rsqrt(piv[0, 0])
        for m in range(1, ROWS):
            out = jnp.where(sub == m, line[m] * lax.rsqrt(piv[m, m]), out)
        if k + 1 + NEAR < groups:
            far = rank_update(out)
            for g in range(k + 1 + NEAR, groups):
                rows[g] = jnp.where(inside, 0.0, rows[g]) - far[ROWS * g : ROWS * g + ROWS, :]
        store(k, jnp.where(lane < first + ROWS, out, 0.0))
        hook(groups - 1 - k)


class Queue:
    def __init__(self):
        self.work = []

    def add(self, task):
        self.work.append(task)

    def some(self, left):
        for _ in range(-(-len(self.work) // (left + 1))):
            self.work.pop(0)()

    def all(self):
        while self.work:
            self.work.pop(0)()


def factorize(a, low, inv, queue, after):
    size = a.shape[0] // PARTS

    def at(i, count=1):
        return slice(i * size, (i + count) * size)

    for k in range(PARTS):
        def store(g, value, k=k):
            inv[k * size + ROWS * g : k * size + ROWS * g + ROWS, :] = value

        rows = [a[k * size + ROWS * g : k * size + ROWS * g + ROWS, at(k)] for g in range(size // ROWS)]
        invert_factor(rows, store, queue.some)
        queue.all()
        if k + 1 < PARTS:
            block = exact(a[at(k + 1), at(k)], inv[at(k), :], NT)
            low[at(k + 1), at(k)] = block
            a[at(k + 1), at(k + 1)] = a[at(k + 1), at(k + 1)] - exact(block, block, NT)
        rest = PARTS - k - 2
        if rest > 0:
            def solve(k=k, rest=rest):
                low[at(k + 2, rest), at(k)] = exact(a[at(k + 2, rest), at(k)], inv[at(k), :], NT)

            queue.add(solve)
            for i in range(k + 1, PARTS):
                def trail(k=k, i=i):
                    j = max(i, k + 2)
                    many = at(j, PARTS - j)
                    a[many, at(i)] = a[many, at(i)] - exact(low[many, at(k)], low[at(i), at(k)], NT)

                queue.add(trail)
        after(k)


def packed_blocks():
    order = []
    for j in range(PARTS):
        if j % 2 == 0:
            order.append(("pair", j))
        order += [("block", i, j) for i in range(j + 1, PARTS)]
    return order


def lower_mask(size):
    row = lax.broadcasted_iota(jnp.int32, (size, size), 0)
    col = lax.broadcasted_iota(jnp.int32, (size, size), 1)
    return row, col


def schur_kernel(rt, proj, diag, rhs, keep, send, full, pack):
    me = lax.axis_index("scen")
    link, share = rt.shape[0], diag.shape[0]
    size = link // PARTS
    for i in range(PARTS):
        upto = (i + 1) * size
        full[i * size : upto, :upto] = dot(rt[i * size : upto, :], rt[:upto, :], NT)
        if i + 1 < PARTS:
            full[i * size : upto, upto:] = jnp.zeros((size, link - upto), F32)
    mine = pl.ds(pl.multiple_of(me * share, ROWS), share)
    full[mine, :] = full[mine, :] + diag[...]
    vec = dot(proj[...].astype(BF16), rt[...], NT) + rhs[...]
    row, col = lower_mask(size)
    order = packed_blocks()
    half = len(order) // 2
    spare = []

    def block(i, j):
        return full[i * size : (i + 1) * size, j * size : (j + 1) * size]

    for n, entry in enumerate(order):
        if entry[0] == "pair":
            j = entry[1]
            second = block(j + 1, j + 1)
            value = jnp.where(row >= col, block(j, j), second)
            spare.append(jnp.sum(jnp.where(row == col, second, 0.0), axis=0, keepdims=True))
        else:
            value = block(entry[1], entry[2])
        pack[n // half, (n % half) * size : (n % half + 1) * size, :] = value
    pack[0, half * size :, :] = jnp.concatenate([vec[:, j * size : (j + 1) * size] for j in range(PARTS)], 0)
    spare.append(jnp.zeros((2 * PARTS - len(spare), size), F32))
    pack[1, half * size :, :] = jnp.concatenate(spare, 0)
    core = lax.rem(me, 2)
    keep[...] = pack[core]
    send[...] = pack[1 - core]


def node_kernel(mine, other, *refs):
    pieces, refs = refs[: refs_pieces(refs)], refs[refs_pieces(refs) :]
    strip, wide, low, inv, wz, a, link_full, acc, sems = refs
    me = lax.axis_index("scen")
    share, link = pieces[0].shape
    size = link // PARTS
    copies = []
    for p, piece in enumerate(pieces):
        start = pl.multiple_of(lax.bitwise_xor(me, p) * share, ROWS)
        copies.append(pltpu.make_async_copy(piece, link_full.at[pl.ds(start, share), :], sems.at[p]))
        copies[-1].start()
    core = lax.rem(me, 2)
    order = packed_blocks()
    half = len(order) // 2
    row, col = lower_mask(size)

    def part(n, r0, r1):
        want = jnp.full((r1 - r0, size), n // half, jnp.int32) == core
        r0, r1 = (n % half) * size + r0, (n % half) * size + r1
        return jnp.where(want, mine[r0:r1, :], other[r0:r1, :])

    def at(i, count=1):
        return slice(i * size, (i + count) * size)

    vec = part(half - 1, size, size + 2 * PARTS)
    spare = part(2 * half - 1, size, size + 2 * PARTS)
    pairs = 0
    for n, entry in enumerate(order):
        if entry[0] == "pair":
            j = entry[1]
            both = part(n, 0, size)
            flip = both.T
            a[at(j), at(j)] = jnp.where(row >= col, both, flip)
            edge = jnp.broadcast_to(spare[pairs : pairs + 1, :], (size, size))
            a[at(j + 1), at(j + 1)] = jnp.where(row == col, edge, jnp.where(row < col, both, flip))
            pairs += 1
        else:
            a[at(entry[1]), at(entry[2])] = part(n, 0, size)
    pad = jnp.zeros((ROWS - 2, size), F32)
    z = [jnp.concatenate([vec[2 * j : 2 * j + 2, :], pad], 0) for j in range(PARTS)]
    for copy in copies:
        copy.wait()
    queue = Queue()
    strip_of = lax.div(me * share, size)
    lanes = [pl.ds(pl.multiple_of(lax.rem(strip_of + PARTS - d, PARTS) * size, size), size) for d in range(3)]
    rz = {0: z[0]}

    def after(k):
        def spread():
            wide[at(k), :] = exact(inv[at(k), :], link_full[at(k), :], NN)

        def vector():
            wz[:, at(k)] = exact(rz[k], inv[at(k), :], NT)

        def products(d):
            def run():
                term = exact(wide[at(k), lanes[0]], wide[at(k), lanes[d]], TN)
                acc[at(d), :] = term if k == 0 else acc[at(d), :] + term
            return run

        def right():
            term = exact(wz[:, at(k)], wide[at(k), lanes[0]], NN)
            acc[3 * size :, :] = term if k == 0 else acc[3 * size :, :] + term

        def coming():
            link_full[at(k + 1), :] = link_full[at(k + 1), :] - exact(low[at(k + 1), at(0, k + 1)], wide[at(0, k + 1), :], NN)
            rz[k + 1] = z[k + 1] - exact(wz[:, at(0, k + 1)], low[at(k + 1), at(0, k + 1)], NT)

        for task in (spread, vector, products(0), products(1), products(2), right):
            queue.add(task)
        if k + 1 < PARTS:
            queue.add(coming)

    factorize(a, low, inv, queue, after)
    queue.all()
    own, above, cross = acc[at(0), :], acc[at(1), :], acc[at(2), :]
    mixed = jnp.where(row >= col, own, cross)
    edge = jnp.sum(jnp.where(row == col, cross, 0.0), axis=0, keepdims=True)
    tail = lax.broadcasted_iota(jnp.int32, (ROWS, size), 0)
    if share == size:
        strip[:share, :] = above
        strip[share : 2 * share, :] = mixed
    else:
        acc[at(0), :] = mixed
        inner = pl.multiple_of(lax.rem(me * share, size), ROWS)
        strip[:share, :] = acc[pl.ds(size + inner, share), :]
        strip[share : 2 * share, :] = acc[pl.ds(inner, share), :]
    strip[2 * share :, :] = jnp.where(tail == 2, jnp.broadcast_to(edge, (ROWS, size)), acc[3 * size :, :])


def refs_pieces(refs):
    return len(refs) - 9


def root_kernel(*refs):
    count = len(refs) - 26
    pieces, refs = refs[:count], refs[count:]
    root_diag, root_rhs, proj, wide_h, low_h, inv_h, wz_h, rt_h, factor_h, leaf, node, root = refs[:12]
    wide, nlow, ninv, nwz, rt, factor, a, low, inv, strips, mixes, ends, whole, sems = refs[12:]
    me = lax.axis_index("scen")
    link = root_diag.shape[0]
    size = link // PARTS
    share = (pieces[0].shape[0] - ROWS) // 2
    copies = []
    for n, (src, dst) in enumerate(((low_h, nlow), (inv_h, ninv), (wide_h, wide), (wz_h, nwz), (rt_h, rt), (factor_h, factor))):
        copies.append(pltpu.make_async_copy(src, dst, sems.at[n]))
        copies[-1].start()

    def at(i, count=1):
        return slice(i * size, (i + count) * size)

    for p, piece in enumerate(pieces):
        who = lax.bitwise_xor(me, p)
        rows = pl.ds(pl.multiple_of(who * share, ROWS), share)
        strips[rows, :] = piece[:share, :]
        mixes[rows, :] = piece[share : 2 * share, :]
        ends[pl.ds(pl.multiple_of(lax.div(who * share, size) * ROWS, ROWS), ROWS), :] = piece[2 * share :, :]
    row, col = lower_mask(size)
    flips = []
    for i in range(PARTS):
        mix = mixes[at(i), :]
        flips.append(mix.T)
        a[at(i), at(i)] = jnp.where(row >= col, mix, flips[i]) + root_diag[at(i), at(i)]
        if i > 0:
            a[at(i), at(i - 1)] = strips[at(i), :] + root_diag[at(i), at(i - 1)]
    a[at(3), at(0)] = strips[at(0), :].T + root_diag[at(3), at(0)]
    for i in (2, 3):
        edge = jnp.broadcast_to(ends[ROWS * i + 2 : ROWS * i + 3, :], (size, size))
        a[at(i), at(i - 2)] = jnp.where(row == col, edge, jnp.where(row < col, mixes[at(i), :], flips[i - 2])) + root_diag[at(i), at(i - 2)]
    pad = jnp.zeros((ROWS - 2, size), F32)
    rhs = [jnp.concatenate([ends[ROWS * i : ROWS * i + 2, :] - root_rhs[:, at(i)], pad], 0) for i in range(PARTS)]
    for copy in copies:
        copy.wait()
    queue = Queue()
    u = {}

    def after(k):
        def forward():
            r = rhs[k]
            for j in range(k):
                r = r - exact(u[j], low[at(k), at(j)], NT)
            u[k] = exact(r, inv[at(k), :], NT)

        queue.add(forward)

    factorize(a, low, inv, queue, after)
    queue.all()
    x = {}
    for k in reversed(range(PARTS)):
        r = u[k]
        for j in range(k + 1, PARTS):
            r = r - exact(x[j], low[at(j), at(k)], NN)
        x[k] = exact(r, inv[at(k), :], NN)
        root[:, at(k)] = x[k][:2, :]
    x0 = jnp.concatenate([x[k] for k in range(PARTS)], 1)
    t = nwz[...] - exact(x0, wide[...], NT)
    xn = {}
    for k in reversed(range(PARTS)):
        r = t[:, at(k)]
        for j in range(k + 1, PARTS):
            r = r - exact(xn[j], nlow[at(j), at(k)], NN)
        xn[k] = exact(r, ninv[at(k), :], NN)
    solved = jnp.concatenate([xn[k] for k in range(PARTS)], 1)
    whole[...] = solved
    if node.shape[1] == size:
        node[...] = whole[:2, pl.ds(pl.multiple_of(me * share, size), size)]
    else:
        node[...] = whole[:2, :]
    update = dot(solved.astype(BF16), rt[...], NN)
    difference = (update[:2, :] - proj[...]).astype(BF16)
    leaf[...] = dot(difference, factor[...], NT)


def swap(x, axis, count, bit):
    return lax.ppermute(x, axis, [(i, i ^ bit) for i in range(count)])


def bits(count, low=1):
    step = low
    while step < count:
        yield step
        step *= 2


def spread(pieces, axis, count, steps):
    for bit in steps:
        for p in list(pieces):
            pieces[p ^ bit] = swap(pieces[p], axis, count, bit)
    return pieces


def build(scen, node):
    vmem = pl.BlockSpec(memory_space=pltpu.VMEM)
    anywhere = pl.BlockSpec(memory_space=pl.ANY)

    def local(factors, couple, leaf_rhs, node_diag, node_rhs, link_root, root_diag, root_rhs):
        factor, coupling, rights = factors[0, 0], couple[0, 0], leaf_rhs[0, 0]
        order, link = coupling.shape
        share = node_diag.shape[1]
        size = link // PARTS
        me = lax.axis_index("scen")
        down = list(reversed(list(bits(scen))))
        links = spread({0: link_root[0]}, "scen", scen, down)
        rt = lax.dot_general(coupling, factor, (TN, ((), ())), preferred_element_type=F32).astype(BF16)
        projected = jnp.dot(rights, factor, preferred_element_type=F32)
        rhs = lax.dynamic_update_slice(jnp.zeros((2, link), F32), node_rhs[0], (0, me * share))
        tall = PARTS * size + 2 * PARTS
        flat = jax.ShapeDtypeStruct((tall, size), F32)
        keep, send = pl.pallas_call(
            schur_kernel,
            out_shape=(flat, flat),
            in_specs=[vmem] * 4,
            out_specs=(vmem, vmem),
            scratch_shapes=[pltpu.VMEM((link, link), F32), pltpu.VMEM((2, tall, size), F32)],
            name="schur",
        )(rt, projected, node_diag[0], rhs)
        mine = keep + swap(send, "scen", scen, 1)
        for bit in bits(scen, 2):
            mine = mine + swap(mine, "scen", scen, bit)
        other = swap(mine, "scen", scen, 1)
        square = jax.ShapeDtypeStruct((link, link), F32)
        strip, wide, low, inv, wz = pl.pallas_call(
            node_kernel,
            out_shape=(
                jax.ShapeDtypeStruct((2 * share + ROWS, size), F32),
                square,
                square,
                jax.ShapeDtypeStruct((link, size), F32),
                jax.ShapeDtypeStruct((ROWS, link), F32),
            ),
            in_specs=[vmem, vmem] + [anywhere] * scen,
            out_specs=(vmem,) * 5,
            scratch_shapes=[
                pltpu.VMEM((link, link), F32),
                pltpu.VMEM((link, link), F32),
                pltpu.VMEM((3 * size + ROWS, size), F32),
                pltpu.SemaphoreType.DMA((scen,)),
            ],
            name="node",
        )(mine, other, *[links[p] for p in range(scen)])
        for bit in bits(node):
            strip = strip + swap(strip, "node", node, bit)
        strips = spread({0: strip}, "scen", scen, down)
        aligned = share % size == 0
        leaf, solved, root = pl.pallas_call(
            root_kernel,
            out_shape=(
                jax.ShapeDtypeStruct((2, order), F32),
                jax.ShapeDtypeStruct((2, share if aligned else link), F32),
                jax.ShapeDtypeStruct((2, link), F32),
            ),
            in_specs=[vmem] * (scen + 3) + [anywhere] * 6,
            out_specs=(vmem,) * 3,
            scratch_shapes=[
                pltpu.VMEM((link, link), F32),
                pltpu.VMEM((link, link), F32),
                pltpu.VMEM((link, size), F32),
                pltpu.VMEM((ROWS, link), F32),
                pltpu.VMEM((link, order), BF16),
                pltpu.VMEM((order, order), BF16),
                pltpu.VMEM((link, link), F32),
                pltpu.VMEM((link, link), F32),
                pltpu.VMEM((link, size), F32),
                pltpu.VMEM((link, size), F32),
                pltpu.VMEM((link, size), F32),
                pltpu.VMEM((PARTS * ROWS, size), F32),
                pltpu.VMEM((ROWS, link), F32),
                pltpu.SemaphoreType.DMA((6,)),
            ],
            name="root",
        )(*[strips[p] for p in range(scen)], root_diag, root_rhs, projected, wide, low, inv, wz, rt, factor)
        if not aligned:
            solved = lax.dynamic_slice(solved, (0, me * share), (2, share))
        return (leaf[None, None], solved[None], root)

    return local


def solution(mesh):
    placed = (
        P("node", "scen", None, None),
        P("node", "scen", None, None),
        P("node", "scen", None, None),
        P("node", "scen", None),
        P("node", None, "scen"),
        P("node", "scen", None),
        P(),
        P(),
    )
    return jax.shard_map(
        build(mesh.shape["scen"], mesh.shape["node"]),
        mesh=mesh,
        in_specs=placed,
        out_specs=(P("node", "scen", None, None), P("node", None, "scen"), P()),
        check_vma=False,
    )
```

time: 500 us -> 98.8 us (0.20)
  other arithmetic: 264 us -> 1.99 us
  matrix products: 59.5 us -> 5.02 us
  waiting for transfers between devices: 81.1 us -> 31.4 us
  Pallas kernels: 0 us -> 44.3 us
  local copies, waits for them, and re-layouts: 40.2 us -> 2.65 us
  blocking collectives: 30.5 us -> 0 us
  between operations: 19.4 us -> 0.93 us
  starting transfers between devices: 0.12 us -> 12.3 us
    another operation x35 -> x0, other arithmetic: 255 us -> none  [the longest x15 88.6 us: local(): root_lower = jnp.linalg.cholesky(root_matrix + root_diag)]
    psum x2 -> x0, waiting for transfers between devices: 80.3 us -> none  [the longest x1 54.3 us: local(): root_matrix, root_vector = lax.psum((root_part, root_vec), 'node')]
    another operation x68 -> x0, matrix products: 47.3 us -> none  [the longest x14 15.2 us: local(): jax.scipy.linalg.cho_solve((root_lower, True), root_vector - root_rhs.T)]
    pallas_call x0 -> x3, Pallas kernels: none -> 44.3 us  [the longest x1 22.5 us: local(): pl.pallas_call(root_kernel, out_shape=(jax.ShapeDtypeStruct((2, order), F...]
    ppermute x0 -> x12, waiting for transfers between devices: none -> 31.4 us  [swap(): return lax.ppermute(x, axis, [(i, i ^ bit) for i in range(count)])]
    psum x2 -> x0, blocking collectives: 30.5 us -> none  [the longest x1 21.9 us: local(): root_matrix, root_vector = lax.psum((root_part, root_vec), 'node')]
    another operation x35 -> x0, local copies, waits for them, and re-layouts: 25.2 us -> none  [the longest x12 13.5 us: local(): jax.scipy.linalg.cho_solve((root_lower, True), root_vector - root_rhs.T)]
    ppermute x0 -> x12, starting transfers between devices: none -> 12.3 us  [swap(): return lax.ppermute(x, axis, [(i, i ^ bit) for i in range(count)])]
  transfers between devices with their start and end apart: 3 -> 12, of which waited for: 2 -> 9; matrix products, arithmetic and copies ran while one was open for 31% -> 0% of each run, Pallas kernels for 0% -> 0%
where the time goes in v1:
time: 98.8 us; the launch traced here: 98.6 us
  Pallas kernels  44.3 us (45%)
  waiting for transfers between devices  31.4 us (32%)
  starting transfers between devices  12.3 us (12%)
  matrix products  5.02 us (5%)
  local copies, waits for them, and re-layouts  2.65 us (3%)
  other arithmetic  1.99 us (2%)
    ppermute x12, waiting for transfers between devices, swap(): return lax.ppermute(x, axis, [(i, i ^ bit) for i in range(count)])  31.4 us
    pallas_call x1, Pallas kernels, local(): pl.pallas_call(root_kernel, out_shape=(jax.ShapeDtypeStruct((2, order), F...  22.5 us
    pallas_call x1, Pallas kernels, local(): pl.pallas_call(node_kernel, out_shape=(jax.ShapeDtypeStruct((2 * share +...  18.5 us
    ppermute x12, starting transfers between devices, swap(): return lax.ppermute(x, axis, [(i, i ^ bit) for i in range(count)])  12.3 us
    pallas_call x1, Pallas kernels, local(): pl.pallas_call(schur_kernel, out_shape=(flat, flat), in_specs=[vmem] * 4,...  3.4 us
    dot_general x1, matrix products, local(): projected = jnp.dot(rights, factor, preferred_element_type=F32)  2.73 us
    unnamed x28, local copies, waits for them, and re-layouts  2.64 us
    dot_general x1, matrix products, local(): lax.dot_general(coupling, factor, (TN, ((), ())), preferred_element_type=...  2.28 us
  transfers between devices with their start and end apart: 12, of which 9 were waited for; matrix products, arithmetic and copies ran while one was open for 0% of the time, Pallas kernels for 0%

profile of v1, /device:TPU:0, one launch (start us, length us, event | category | flops | bytes accessed | tf_op | source)
XLA Modules:
  0.0 98.6 jit_solution(3347079900115277548)
XLA Ops:
  0.7 2.7 %fusion.1.proj.refs_6_ = f32[2,1024]{1,0:T(2,128)} fusion(bf16[1,1,2,1024]{3,2,1,0:T(2,128)(2,1)} %param.10, bf16[1,1,1024,1024]{3,2,1,0:T(8,128)(2,1)} %param.8), kind=kOutput, calls=%fused_computation.2 | convolution fusion | flops 4194304 | bytes 2109440 | tf_op jit(solution)/shard_map/dot_general | solution.py:396
  3.4 2.3 %convolution_convert_fusion.rt.refs_11_ = bf16[512,1024]{1,0:T(8,128)(2,1)} fusion(bf16[1,1,1024,512]{3,2,1,0:T(8,128)(2,1)S(1)} %copy-done, bf16[1,1,1024,1024]{3,2,1,0:T(8,128)(2,1)S(1)} %copy-done.1), kind=kOutput, calls=%fused_computation | convolution fusion | flops 1074266112 | bytes 4194304 | tf_op jit(solution)/shard_map/dot_general | solution.py:395
  6.3 3.4 %schur.1 = (f32[520,128]{1,0:T(8,128)}, f32[520,128]{1,0:T(8,128)}) custom-call(bf16[512,1024]{1,0:T(8,128)(2,1)} %convolution_convert_fusion.rt.refs_11_, f32[2,1024]{1,0:T(2,128)} %fusion.1.proj.refs_6_, f32[128,512]{1,0:T(8,128)} %bitcast.18, f32[2,512]{1,0:T(2,128)} %copy-done.12), custom_call_target="tpu_custom_call" | custom-call | tf_op jit(solution)/shard_map/schur/pallas_call | solution.py:400
  10.2 1.4 %collective-permute-done = f32[520,128]{1,0:T(8,128)S(1)} collective-permute-done((f32[520,128]{1,0:T(8,128)}, f32[520,128]{1,0:T(8,128)S(1)}, u32[]{:S(2)}, u32[]{:S(2)}) %collective-permute-start) | collective-permute-done | bytes 266272 | tf_op jit(solution)/shard_map/ppermute | solution.py:366
  11.6 1.0 %add.19 = f32[520,128]{1,0:T(8,128)S(1)} add(f32[520,128]{1,0:T(8,128)} %get-tuple-element.13, f32[520,128]{1,0:T(8,128)S(1)} %collective-permute-done) | non-fusion elementwise | flops 66560 | bytes 798720 | tf_op jit(solution)/shard_map/add | solution.py:408
  12.6 2.9 %collective-permute-start.1 = (f32[520,128]{1,0:T(8,128)S(1)}, f32[520,128]{1,0:T(8,128)S(1)}, u32[]{:S(2)}, u32[]{:S(2)}) collective-permute-start(f32[520,128]{1,0:T(8,128)S(1)} %add.19), channel_id=1, source_target_pairs={{0,16},{8,24},{16,0},{24,8},{1,17},{9,25},{17,1},{25,9},{2,18},{10... | collective-permute-start | bytes 798728 | tf_op jit(solution)/shard_map/ppermute | solution.py:366
  15.6 7.2 %collective-permute-done.1 = f32[520,128]{1,0:T(8,128)S(1)} collective-permute-done((f32[520,128]{1,0:T(8,128)S(1)}, f32[520,128]{1,0:T(8,128)S(1)}, u32[]{:S(2)}, u32[]{:S(2)}) %collective-permute-start.1) | collective-permute-done | bytes 266272 | tf_op jit(solution)/shard_map/ppermute | solution.py:366
  23.4 4.4 %collective-permute-done.4.refs_2_ = f32[128,512]{1,0:T(8,128)S(1)} collective-permute-done((f32[128,512]{1,0:T(8,128)S(1)}, f32[128,512]{1,0:T(8,128)S(1)}, u32[]{:S(2)}, u32[]{:S(2)}) %collective-permute-start.4) | collective-permute-done | bytes 262176 | tf_op jit(solution)/shard_map/ppermute | solution.py:366
  27.8 1.5 %collective-permute-done.5.refs_3_ = f32[128,512]{1,0:T(8,128)S(1)} collective-permute-done((f32[128,512]{1,0:T(8,128)S(1)}, f32[128,512]{1,0:T(8,128)S(1)}, u32[]{:S(2)}, u32[]{:S(2)}) %collective-permute-start.5) | collective-permute-done | bytes 262176 | tf_op jit(solution)/shard_map/ppermute | solution.py:366
  29.4 0.7 copy-done.8
  30.1 0.7 copy-done.4
  30.8 18.5 %node.1 = (f32[264,128]{1,0:T(8,128)}, f32[512,512]{1,0:T(8,128)}, f32[512,512]{1,0:T(8,128)}, f32[512,128]{1,0:T(8,128)}, f32[8,512]{1,0:T(8,128)}) custom-call(f32[520,128]{1,0:T(8,128)} %copy-done.2, f32[520,128]{1,0:T(8,128)} %copy-done.4, f32[128,512]{1,0:T(8,128)} %bitcast.19, f32[128,512]{1,0:T(8,128)} %copy-done.7, f32[128,512]{1,0:T(8,128)} %copy-done.6, ...), custom_call_target="tpu_custom_call" | custom-call | tf_op jit(solution)/shard_map/node/pallas_call | solution.py:413
  49.2 1.8 %collective-permute-start.6 = (f32[264,128]{1,0:T(8,128)}, f32[264,128]{1,0:T(8,128)S(1)}, u32[]{:S(2)}, u32[]{:S(2)}) collective-permute-start(f32[264,128]{1,0:T(8,128)} %get-tuple-element.15), channel_id=1, source_target_pairs={{0,1},{1,0},{2,3},{3,2},{4,5},{5,4},{6,7},{7,6},{8,9},{9,8},{10,11... | collective-permute-start | bytes 405512 | tf_op jit(solution)/shard_map/ppermute | solution.py:366
  51.0 4.1 %collective-permute-done.6 = f32[264,128]{1,0:T(8,128)S(1)} collective-permute-done((f32[264,128]{1,0:T(8,128)}, f32[264,128]{1,0:T(8,128)S(1)}, u32[]{:S(2)}, u32[]{:S(2)}) %collective-permute-start.6) | collective-permute-done | bytes 135200 | tf_op jit(solution)/shard_map/ppermute | solution.py:366
  55.1 0.9 add.21
  56.1 1.9 %collective-permute-start.7 = (f32[264,128]{1,0:T(8,128)S(1)}, f32[264,128]{1,0:T(8,128)S(1)}, u32[]{:S(2)}, u32[]{:S(2)}) collective-permute-start(f32[264,128]{1,0:T(8,128)S(1)} %add.21), channel_id=1, source_target_pairs={{0,2},{1,3},{2,0},{3,1},{4,6},{5,7},{6,4},{7,5},{8,10},{9,11},{10,... | collective-permute-start | bytes 405512 | tf_op jit(solution)/shard_map/ppermute | solution.py:366
  57.9 3.2 %collective-permute-done.7 = f32[264,128]{1,0:T(8,128)S(1)} collective-permute-done((f32[264,128]{1,0:T(8,128)S(1)}, f32[264,128]{1,0:T(8,128)S(1)}, u32[]{:S(2)}, u32[]{:S(2)}) %collective-permute-start.7) | collective-permute-done | bytes 135200 | tf_op jit(solution)/shard_map/ppermute | solution.py:366
  61.2 2.9 %collective-permute-start.8 = (f32[264,128]{1,0:T(8,128)S(1)}, f32[264,128]{1,0:T(8,128)S(1)}, u32[]{:S(2)}, u32[]{:S(2)}) collective-permute-start(f32[264,128]{1,0:T(8,128)S(1)} %add.22), channel_id=1, source_target_pairs={{0,4},{1,5},{2,6},{3,7},{4,0},{5,1},{6,2},{7,3},{8,12},{9,13},{10,... | collective-permute-start | bytes 405512 | tf_op jit(solution)/shard_map/ppermute | solution.py:366
  64.0 4.8 %collective-permute-done.8 = f32[264,128]{1,0:T(8,128)S(1)} collective-permute-done((f32[264,128]{1,0:T(8,128)S(1)}, f32[264,128]{1,0:T(8,128)S(1)}, u32[]{:S(2)}, u32[]{:S(2)}) %collective-permute-start.8) | collective-permute-done | bytes 135200 | tf_op jit(solution)/shard_map/ppermute | solution.py:366
  68.8 1.6 %collective-permute-start.10 = (f32[264,128]{1,0:T(8,128)S(1)}, f32[264,128]{1,0:T(8,128)S(1)}, u32[]{:S(2)}, u32[]{:S(2)}) collective-permute-start(f32[264,128]{1,0:T(8,128)S(1)} %add.23.refs_0_), channel_id=1, source_target_pairs={{0,16},{8,24},{16,0},{24,8},{1,17},{9,25},{17,1},{25,9},{2,18},{10... | collective-permute-start | bytes 405512 | tf_op jit(solution)/shard_map/ppermute | solution.py:366
  70.5 3.4 %collective-permute-done.10.refs_2_ = f32[264,128]{1,0:T(8,128)S(1)} collective-permute-done((f32[264,128]{1,0:T(8,128)S(1)}, f32[264,128]{1,0:T(8,128)S(1)}, u32[]{:S(2)}, u32[]{:S(2)}) %collective-permute-start.10) | collective-permute-done | bytes 135200 | tf_op jit(solution)/shard_map/ppermute | solution.py:366
  73.9 1.3 %collective-permute-done.11.refs_3_ = f32[264,128]{1,0:T(8,128)S(1)} collective-permute-done((f32[264,128]{1,0:T(8,128)S(1)}, f32[264,128]{1,0:T(8,128)S(1)}, u32[]{:S(2)}, u32[]{:S(2)}) %collective-permute-start.11) | collective-permute-done | bytes 135200 | tf_op jit(solution)/shard_map/ppermute | solution.py:366
  75.3 0.6 copy-done.11
  75.9 22.5 %root.1 = (f32[2,1024]{1,0:T(2,128)}, f32[2,128]{1,0:T(2,128)}, f32[2,512]{1,0:T(2,128)}) custom-call(f32[264,128]{1,0:T(8,128)} %copy-done.3, f32[264,128]{1,0:T(8,128)} %copy-done.10, f32[264,128]{1,0:T(8,128)} %copy-done.9, f32[264,128]{1,0:T(8,128)} %copy-done.11, f32[512,512]{1,0:T(8,128)} %refs_4_.1, f32[2,512]{1,0:T(2,128)} %refs_5_.1, ...), custom_call_target="tpu_custom_call" | custom-call | tf_op jit(solution)/shard_map/root/pallas_call | solution.py:436
  (40 shorter events, 1.9 us)
Async XLA Ops:
  0.6 2.8 %copy-start = (bf16[1,1,1024,512]{3,2,1,0:T(8,128)(2,1)S(1)}, bf16[1,1,1024,512]{3,2,1,0:T(8,128)(2,1)}, u32[]{:S(2)}) copy-start(bf16[1,1,1024,512]{3,2,1,0:T(8,128)(2,1)} %param.9) | copy-start | bytes 3145732
  0.6 2.8 %copy-start.1 = (bf16[1,1,1024,1024]{3,2,1,0:T(8,128)(2,1)S(1)}, bf16[1,1,1024,1024]{3,2,1,0:T(8,128)(2,1)}, u32[]{:S(2)}) copy-start(bf16[1,1,1024,1024]{3,2,1,0:T(8,128)(2,1)} %param.8) | copy-start | bytes 6291460
  3.4 2.3 %copy-start.13 = (f32[1,2,128]{2,1,0:T(2,128)S(1)}, f32[1,2,128]{2,1,0:T(2,128)}, u32[]{:S(2)}) copy-start(f32[1,2,128]{2,1,0:T(2,128)} %param.12) | copy-start | bytes 3076
  5.7 9.8 %copy-start.5 = (f32[1,128,512]{2,1,0:T(8,128)S(1)}, f32[1,128,512]{2,1,0:T(8,128)}, u32[]{:S(2)}) copy-start(f32[1,128,512]{2,1,0:T(8,128)} %param.13) | copy-start | bytes 786436
  9.7 1.9 %collective-permute-start = (f32[520,128]{1,0:T(8,128)}, f32[520,128]{1,0:T(8,128)S(1)}, u32[]{:S(2)}, u32[]{:S(2)}) collective-permute-start(f32[520,128]{1,0:T(8,128)} %get-tuple-element.14), channel_id=1, source_target_pairs={{0,8},{8,0},{16,24},{24,16},{1,9},{9,1},{17,25},{25,17},{2,10},{10... | collective-permute-start | bytes 798728 | tf_op jit(solution)/shard_map/ppermute | solution.py:366
  12.6 10.2 %collective-permute-start.1 = (f32[520,128]{1,0:T(8,128)S(1)}, f32[520,128]{1,0:T(8,128)S(1)}, u32[]{:S(2)}, u32[]{:S(2)}) collective-permute-start(f32[520,128]{1,0:T(8,128)S(1)} %add.19), channel_id=1, source_target_pairs={{0,16},{8,24},{16,0},{24,8},{1,17},{9,25},{17,1},{25,9},{2,18},{10... | collective-permute-start | bytes 798728 | tf_op jit(solution)/shard_map/ppermute | solution.py:366
  15.5 12.3 %collective-permute-start.4 = (f32[128,512]{1,0:T(8,128)S(1)}, f32[128,512]{1,0:T(8,128)S(1)}, u32[]{:S(2)}, u32[]{:S(2)}) collective-permute-start(f32[128,512]{1,0:T(8,128)S(1)} %bitcast.20), channel_id=1, source_target_pairs={{0,16},{8,24},{16,0},{24,8},{1,17},{9,25},{17,1},{25,9},{2,18},{10... | collective-permute-start | bytes 786440 | tf_op jit(solution)/shard_map/ppermute | solution.py:366
  22.8 6.6 %copy-start.2 = (f32[520,128]{1,0:T(8,128)}, f32[520,128]{1,0:T(8,128)S(1)}, u32[]{:S(2)}) copy-start(f32[520,128]{1,0:T(8,128)S(1)} %add.20.mine) | copy-start | bytes 798724
  22.8 6.6 %collective-permute-start.2 = (f32[520,128]{1,0:T(8,128)S(1)}, f32[520,128]{1,0:T(8,128)S(1)}, u32[]{:S(2)}, u32[]{:S(2)}) collective-permute-start(f32[520,128]{1,0:T(8,128)S(1)} %add.20.mine), channel_id=1, source_target_pairs={{0,8},{8,0},{16,24},{24,16},{1,9},{9,1},{17,25},{25,17},{2,10},{10... | collective-permute-start | bytes 798728 | tf_op jit(solution)/shard_map/ppermute | solution.py:366
  22.9 4.9 %collective-permute-start.3 = (f32[128,512]{1,0:T(8,128)S(1)}, f32[128,512]{1,0:T(8,128)S(1)}, u32[]{:S(2)}, u32[]{:S(2)}) collective-permute-start(f32[128,512]{1,0:T(8,128)S(1)} %bitcast.21), channel_id=1, source_target_pairs={{0,8},{8,0},{16,24},{24,16},{1,9},{9,1},{17,25},{25,17},{2,10},{10... | collective-permute-start | bytes 786440 | tf_op jit(solution)/shard_map/ppermute | solution.py:366
  27.8 1.6 %copy-start.6 = (f32[128,512]{1,0:T(8,128)}, f32[128,512]{1,0:T(8,128)S(1)}, u32[]{:S(2)}) copy-start(f32[128,512]{1,0:T(8,128)S(1)} %collective-permute-done.4.refs_2_) | copy-start | bytes 786436
  27.8 1.5 %collective-permute-start.5 = (f32[128,512]{1,0:T(8,128)S(1)}, f32[128,512]{1,0:T(8,128)S(1)}, u32[]{:S(2)}, u32[]{:S(2)}) collective-permute-start(f32[128,512]{1,0:T(8,128)S(1)} %collective-permute-done.4.refs_2_), channel_id=1, source_target_pairs={{0,8},{8,0},{16,24},{24,16},{1,9},{9,1},{17,25},{25,17},{2,10},{10... | collective-permute-start | bytes 786440 | tf_op jit(solution)/shard_map/ppermute | solution.py:366
  27.8 1.6 %copy-start.7 = (f32[128,512]{1,0:T(8,128)}, f32[128,512]{1,0:T(8,128)S(1)}, u32[]{:S(2)}) copy-start(f32[128,512]{1,0:T(8,128)S(1)} %collective-permute-done.3.refs_1_) | copy-start | bytes 786436
  29.4 0.7 copy-start.8
  30.1 0.7 copy-start.4
  49.2 5.9 %collective-permute-start.6 = (f32[264,128]{1,0:T(8,128)}, f32[264,128]{1,0:T(8,128)S(1)}, u32[]{:S(2)}, u32[]{:S(2)}) collective-permute-start(f32[264,128]{1,0:T(8,128)} %get-tuple-element.15), channel_id=1, source_target_pairs={{0,1},{1,0},{2,3},{3,2},{4,5},{5,4},{6,7},{7,6},{8,9},{9,8},{10,11... | collective-permute-start | bytes 405512 | tf_op jit(solution)/shard_map/ppermute | solution.py:366
  56.1 5.1 %collective-permute-start.7 = (f32[264,128]{1,0:T(8,128)S(1)}, f32[264,128]{1,0:T(8,128)S(1)}, u32[]{:S(2)}, u32[]{:S(2)}) collective-permute-start(f32[264,128]{1,0:T(8,128)S(1)} %add.21), channel_id=1, source_target_pairs={{0,2},{1,3},{2,0},{3,1},{4,6},{5,7},{6,4},{7,5},{8,10},{9,11},{10,... | collective-permute-start | bytes 405512 | tf_op jit(solution)/shard_map/ppermute | solution.py:366
  61.2 7.7 %collective-permute-start.8 = (f32[264,128]{1,0:T(8,128)S(1)}, f32[264,128]{1,0:T(8,128)S(1)}, u32[]{:S(2)}, u32[]{:S(2)}) collective-permute-start(f32[264,128]{1,0:T(8,128)S(1)} %add.22), channel_id=1, source_target_pairs={{0,4},{1,5},{2,6},{3,7},{4,0},{5,1},{6,2},{7,3},{8,12},{9,13},{10,... | collective-permute-start | bytes 405512 | tf_op jit(solution)/shard_map/ppermute | solution.py:366
  68.8 6.4 %copy-start.3 = (f32[264,128]{1,0:T(8,128)}, f32[264,128]{1,0:T(8,128)S(1)}, u32[]{:S(2)}) copy-start(f32[264,128]{1,0:T(8,128)S(1)} %add.23.refs_0_) | copy-start | bytes 405508
  68.8 5.1 %collective-permute-start.10 = (f32[264,128]{1,0:T(8,128)S(1)}, f32[264,128]{1,0:T(8,128)S(1)}, u32[]{:S(2)}, u32[]{:S(2)}) collective-permute-start(f32[264,128]{1,0:T(8,128)S(1)} %add.23.refs_0_), channel_id=1, source_target_pairs={{0,16},{8,24},{16,0},{24,8},{1,17},{9,25},{17,1},{25,9},{2,18},{10... | collective-permute-start | bytes 405512 | tf_op jit(solution)/shard_map/ppermute | solution.py:366
  70.5 3.4 %collective-permute-start.9 = (f32[264,128]{1,0:T(8,128)S(1)}, f32[264,128]{1,0:T(8,128)S(1)}, u32[]{:S(2)}, u32[]{:S(2)}) collective-permute-start(f32[264,128]{1,0:T(8,128)S(1)} %add.23.refs_0_), channel_id=1, source_target_pairs={{0,8},{8,0},{16,24},{24,16},{1,9},{9,1},{17,25},{25,17},{2,10},{10... | collective-permute-start | bytes 405512 | tf_op jit(solution)/shard_map/ppermute | solution.py:366
  73.9 1.4 %copy-start.9 = (f32[264,128]{1,0:T(8,128)}, f32[264,128]{1,0:T(8,128)S(1)}, u32[]{:S(2)}) copy-start(f32[264,128]{1,0:T(8,128)S(1)} %collective-permute-done.10.refs_2_) | copy-start | bytes 405508
  73.9 1.4 %collective-permute-start.11 = (f32[264,128]{1,0:T(8,128)S(1)}, f32[264,128]{1,0:T(8,128)S(1)}, u32[]{:S(2)}, u32[]{:S(2)}) collective-permute-start(f32[264,128]{1,0:T(8,128)S(1)} %collective-permute-done.10.refs_2_), channel_id=1, source_target_pairs={{0,8},{8,0},{16,24},{24,16},{1,9},{9,1},{17,25},{25,17},{2,10},{10... | collective-permute-start | bytes 405512 | tf_op jit(solution)/shard_map/ppermute | solution.py:366
  73.9 1.4 %copy-start.10 = (f32[264,128]{1,0:T(8,128)}, f32[264,128]{1,0:T(8,128)S(1)}, u32[]{:S(2)}) copy-start(f32[264,128]{1,0:T(8,128)S(1)} %collective-permute-done.9.refs_1_) | copy-start | bytes 405508
  (2 other events, 1.2 us)

commit v2 on v1

--- a/solution.py
+++ b/solution.py
@@ -9,7 +9,8 @@
 NN, NT, TN = ((1,), (0,)), ((1,), (1,)), ((0,), (0,))
 ROWS = 8
 PARTS = 4
-NEAR = 2
+GRANT = 24 << 20
+PANEL = 16
 
 
 def dot(a, b, dims):
@@ -52,40 +53,56 @@
     shape = rows[0].shape
     lane = lax.broadcasted_iota(jnp.int32, shape, 1)
     sub = lax.broadcasted_iota(jnp.int32, shape, 0)
-    groups = len(rows)
-    for k in range(groups):
+    groups, span = len(rows), PANEL // ROWS
+    for k in range(0, groups, span):
         first = ROWS * k
-        inside = (lane >= first) & (lane < first + ROWS)
-        cols = [from_lane(rows[k], first + i) for i in range(ROWS)]
-        piv = {(m, i): from_row(cols[i], m) for i in range(ROWS) for m in range(i, ROWS)}
-        panel = jnp.where(inside, jnp.where(lane - first == sub, 1.0, 0.0), rows[k])
-        line = [jnp.broadcast_to(panel[i : i + 1, :], shape) for i in range(ROWS)]
-        near = range(k + 1, min(k + 1 + NEAR, groups))
-        mult = {g: [from_lane(rows[g], first + i) for i in range(ROWS)] for g in near}
+        inside = (lane >= first) & (lane < first + PANEL)
+        own = range(k, k + span)
+        near = range(k + span, min(k + 2 * span, groups))
+        both = [*own, *near]
+        cols = {(i, g): from_lane(rows[g], first + i) for i in range(PANEL) for g in both if g >= k + i // ROWS}
+        lines = {g: jnp.where(inside, jnp.where(lane - ROWS * g == sub, 1.0, 0.0), rows[g]) for g in own}
         kept = {g: jnp.where(inside, 0.0, rows[g]) for g in near}
-        for i in range(ROWS):
-            inverse = 1.0 / piv[i, i]
-            ratio = {m: piv[m, i] * inverse for m in range(i + 1, ROWS)}
-            for m in range(i + 1, ROWS):
-                for p in range(i + 1, m + 1):
-                    piv[m, p] = piv[m, p] - ratio[m] * piv[p, i]
-            for m in range(i + 1, ROWS):
-                line[m] = line[m] - ratio[m] * line[i]
+
+        def entry(j, i):
+            return from_row(cols[i, k + j // ROWS], j % ROWS)
+
+        pivots = [entry(0, 0)]
+        for i in range(PANEL):
+            home, at = k + i // ROWS, i % ROWS
+            inverse = 1.0 / pivots[i]
+            if i + 1 < PANEL:
+                below = entry(i + 1, i)
+                pivots.append(entry(i + 1, i + 1) - (below * inverse) * below)
+            ratio = {g: cols[i, g] * inverse for g in both if g >= home}
+            for p in range(i + 1, PANEL):
+                across = entry(p, i)
+                for g in both:
+                    if g >= k + p // ROWS:
+                        cols[p, g] = cols[p, g] - ratio[g] * across
+            line = jnp.broadcast_to(lines[home][at : at + 1, :], shape)
+            for g in own:
+                if g > home:
+                    lines[g] = lines[g] - ratio[g] * line
+                elif g == home and at < ROWS - 1:
+                    lines[g] = lines[g] - jnp.where(sub > at, ratio[g], 0.0) * line
             for g in near:
-                for p in range(i + 1, ROWS):
-                    mult[g][p] = mult[g][p] - mult[g][i] * ratio[p]
-                kept[g] = kept[g] - (mult[g][i] * inverse) * line[i]
+                kept[g] = kept[g] - ratio[g] * line
         for g in near:
             rows[g] = kept[g]
-        out = line[0] * lax.rsqrt(piv[0, 0])
-        for m in range(1, ROWS):
-            out = jnp.where(sub == m, line[m] * lax.rsqrt(piv[m, m]), out)
-        if k + 1 + NEAR < groups:
-            far = rank_update(out)
-            for g in range(k + 1 + NEAR, groups):
+        done = []
+        for o in range(span):
+            pivot = pivots[ROWS * o]
+            for m in range(1, ROWS):
+                pivot = jnp.where(sub == m, pivots[ROWS * o + m], pivot)
+            done.append(lines[k + o] * lax.rsqrt(pivot))
+        if k + 2 * span < groups:
+            far = rank_update(jnp.concatenate(done, 0))
+            for g in range(k + 2 * span, groups):
                 rows[g] = jnp.where(inside, 0.0, rows[g]) - far[ROWS * g : ROWS * g + ROWS, :]
-        store(k, jnp.where(lane < first + ROWS, out, 0.0))
-        hook(groups - 1 - k)
+        for o in range(span):
+            store(k + o, jnp.where(lane - sub <= ROWS * (k + o), done[o], 0.0))
+        hook((groups - k) // span - 1)
 
 
 class Queue:
@@ -152,18 +169,47 @@
     return row, col
 
 
-def schur_kernel(rt, proj, diag, rhs, keep, send, full, pack):
+def schur_kernel(factor_h, couple_h, diag_h, rights_h, rhs_h, rt, proj, keep, send, factor, couple, turned, diag, rights, rhs, full, pack, line, sems):
     me = lax.axis_index("scen")
-    link, share = rt.shape[0], diag.shape[0]
+    order, link = couple.shape
+    share = diag.shape[0]
     size = link // PARTS
-    for i in range(PARTS):
-        upto = (i + 1) * size
-        full[i * size : upto, :upto] = dot(rt[i * size : upto, :], rt[:upto, :], NT)
-        if i + 1 < PARTS:
-            full[i * size : upto, upto:] = jnp.zeros((size, link - upto), F32)
+    width = order // PARTS
+    loads = [pltpu.make_async_copy(couple_h, couple, sems.at[PARTS])]
+    small = ((rights_h, rights), (diag_h, diag), (rhs_h, rhs))
+    small = [pltpu.make_async_copy(src, dst, sems.at[PARTS + 1 + n]) for n, (src, dst) in enumerate(small)]
+    for c in range(PARTS):
+        cut = slice(c * width, (c + 1) * width)
+        loads.append(pltpu.make_async_copy(factor_h.at[:, cut], factor.at[:, cut], sems.at[c]))
+    for load in [*loads, *small]:
+        load.start()
+    loads[0].wait()
+    turned[...] = couple[...].T
+    for c in range(PARTS):
+        cut = slice(c * width, (c + 1) * width)
+        loads[1 + c].wait()
+        rt[:, cut] = dot(turned[...], factor[:, cut], NN).astype(BF16)
+        if c == 0:
+            small[0].wait()
+        proj[:, cut] = dot(rights[...], factor[:, cut], NN)
+        for i in range(PARTS):
+            rows, upto = slice(i * size, (i + 1) * size), (i + 1) * size
+            term = dot(rt[rows, cut], rt[:upto, cut], NT)
+            full[rows, :upto] = term if c == 0 else full[rows, :upto] + term
+    small[1].wait()
+    small[2].wait()
+    for i in range(PARTS - 1):
+        full[i * size : (i + 1) * size, (i + 1) * size :] = jnp.zeros((size, link - (i + 1) * size), F32)
     mine = pl.ds(pl.multiple_of(me * share, ROWS), share)
     full[mine, :] = full[mine, :] + diag[...]
-    vec = dot(proj[...].astype(BF16), rt[...], NT) + rhs[...]
+    vec = dot(proj[...].astype(BF16), rt[...], NT)
+    if rhs.shape[1] == link:
+        vec = vec + rhs[...]
+    else:
+        line[...] = vec
+        mine = pl.ds(pl.multiple_of(me * share, size), share)
+        line[:, mine] = line[:, mine] + rhs[...]
+        vec = line[...]
     row, col = lower_mask(size)
     order = packed_blocks()
     half = len(order) // 2
@@ -380,9 +426,14 @@
     return pieces
 
 
+def hbm(x):
+    return pltpu.with_memory_space_constraint(x, pltpu.HBM)
+
+
 def build(scen, node):
     vmem = pl.BlockSpec(memory_space=pltpu.VMEM)
     anywhere = pl.BlockSpec(memory_space=pl.ANY)
+    far = pl.BlockSpec(memory_space=pltpu.HBM)
 
     def local(factors, couple, leaf_rhs, node_diag, node_rhs, link_root, root_diag, root_rhs):
         factor, coupling, rights = factors[0, 0], couple[0, 0], leaf_rhs[0, 0]
@@ -391,20 +442,39 @@
         size = link // PARTS
         me = lax.axis_index("scen")
         down = list(reversed(list(bits(scen))))
-        links = spread({0: link_root[0]}, "scen", scen, down)
-        rt = lax.dot_general(coupling, factor, (TN, ((), ())), preferred_element_type=F32).astype(BF16)
-        projected = jnp.dot(rights, factor, preferred_element_type=F32)
-        rhs = lax.dynamic_update_slice(jnp.zeros((2, link), F32), node_rhs[0], (0, me * share))
+        links = spread({0: link_root[0]}, "scen", scen, down[:-1])
+        rhs = node_rhs[0]
+        if share % size:
+            rhs = lax.dynamic_update_slice(jnp.zeros((2, link), F32), rhs, (0, me * share))
         tall = PARTS * size + 2 * PARTS
         flat = jax.ShapeDtypeStruct((tall, size), F32)
-        keep, send = pl.pallas_call(
+        rt, projected, keep, send = pl.pallas_call(
             schur_kernel,
-            out_shape=(flat, flat),
-            in_specs=[vmem] * 4,
-            out_specs=(vmem, vmem),
-            scratch_shapes=[pltpu.VMEM((link, link), F32), pltpu.VMEM((2, tall, size), F32)],
+            out_shape=(
+                jax.ShapeDtypeStruct((link, order), BF16),
+                jax.ShapeDtypeStruct((2, order), F32),
+                flat,
+                flat,
+            ),
+            in_specs=[far] * 5,
+            out_specs=(vmem,) * 4,
+            scratch_shapes=[
+                pltpu.VMEM((order, order), BF16),
+                pltpu.VMEM((order, link), BF16),
+                pltpu.VMEM((link, order), BF16),
+                pltpu.VMEM((share, link), F32),
+                pltpu.VMEM((2, order), BF16),
+                pltpu.VMEM(rhs.shape, F32),
+                pltpu.VMEM((link, link), F32),
+                pltpu.VMEM((2, tall, size), F32),
+                pltpu.VMEM((2, link), F32),
+                pltpu.SemaphoreType.DMA((PARTS + 4,)),
+            ],
             name="schur",
-        )(rt, projected, node_diag[0], rhs)
+            compiler_params=pltpu.CompilerParams(vmem_limit_bytes=GRANT),
+        )(*[hbm(x) for x in (factor, coupling, node_diag[0], rights, rhs)])
+        send, links = lax.optimization_barrier((send, links))
+        links = spread(links, "scen", scen, down[-1:])
         mine = keep + swap(send, "scen", scen, 1)
         for bit in bits(scen, 2):
             mine = mine + swap(mine, "scen", scen, bit)
@@ -428,6 +498,7 @@
                 pltpu.SemaphoreType.DMA((scen,)),
             ],
             name="node",
+            compiler_params=pltpu.CompilerParams(vmem_limit_bytes=GRANT),
         )(mine, other, *[links[p] for p in range(scen)])
         for bit in bits(node):
             strip = strip + swap(strip, "node", node, bit)
@@ -459,6 +530,7 @@
                 pltpu.SemaphoreType.DMA((6,)),
             ],
             name="root",
+            compiler_params=pltpu.CompilerParams(vmem_limit_bytes=GRANT),
         )(*[strips[p] for p in range(scen)], root_diag, root_rhs, projected, wide, low, inv, wz, rt, factor)
         if not aligned:
             solved = lax.dynamic_slice(solved, (0, me * share), (2, share))

time: 98.8 us -> 74.5 us (0.75)
  Pallas kernels: 44.3 us -> 33.1 us
  matrix products: 5.02 us -> 0 us
  waiting for transfers between devices: 31.4 us -> 26.9 us
  local copies, waits for them, and re-layouts: 2.65 us -> 0.01 us
  other arithmetic: 1.99 us -> 0.13 us
  starting transfers between devices: 12.3 us -> 13.3 us
    pallas_call x1, Pallas kernels: 22.5 us -> 15.2 us  [local(): pl.pallas_call(root_kernel, out_shape=(jax.ShapeDtypeStruct((2, order), F...]
    pallas_call x1, Pallas kernels: 18.5 us -> 11.4 us  [local(): pl.pallas_call(node_kernel, out_shape=(jax.ShapeDtypeStruct((2 * share +...]
    dot_general x2 -> x0, matrix products: 5.02 us -> none  [the longest x1 2.73 us: local(): projected = jnp.dot(rights, factor, preferred_element_type=F32)]
    ppermute x12, waiting for transfers between devices: 31.4 us -> 26.9 us  [swap(): return lax.ppermute(x, axis, [(i, i ^ bit) for i in range(count)])]
    pallas_call x1, Pallas kernels: 3.4 us -> 6.54 us  [local(): pl.pallas_call(schur_kernel, out_shape=(jax.ShapeDtypeStruct((link, order...]
    unnamed x28 -> x8, local copies, waits for them, and re-layouts: 2.64 us -> 0.01 us
    ppermute x12, starting transfers between devices: 12.3 us -> 13.3 us  [swap(): return lax.ppermute(x, axis, [(i, i ^ bit) for i in range(count)])]
  transfers between devices with their start and end apart: 12 -> 12, of which waited for: 9 -> 9; matrix products, arithmetic and copies ran while one was open for 0% -> 0% of each run, Pallas kernels for 0% -> 9%
where the time goes in v2:
time: 74.5 us; the launch traced here: 74.4 us
  Pallas kernels  33.1 us (44%)
  waiting for transfers between devices  26.9 us (36%)
  starting transfers between devices  13.3 us (18%)
  between operations  0.88 us (1%)
    ppermute x12, waiting for transfers between devices, swap(): return lax.ppermute(x, axis, [(i, i ^ bit) for i in range(count)])  26.9 us
    pallas_call x1, Pallas kernels, local(): pl.pallas_call(root_kernel, out_shape=(jax.ShapeDtypeStruct((2, order), F...  15.2 us
    ppermute x12, starting transfers between devices, swap(): return lax.ppermute(x, axis, [(i, i ^ bit) for i in range(count)])  13.3 us
    pallas_call x1, Pallas kernels, local(): pl.pallas_call(node_kernel, out_shape=(jax.ShapeDtypeStruct((2 * share +...  11.4 us
    pallas_call x1, Pallas kernels, local(): pl.pallas_call(schur_kernel, out_shape=(jax.ShapeDtypeStruct((link, order...  6.54 us
  transfers between devices with their start and end apart: 12, of which 9 were waited for; matrix products, arithmetic and copies ran while one was open for 0% of the time, Pallas kernels for 9%

profile of v2, /device:TPU:0, one launch (start us, length us, event | category | flops | bytes accessed | tf_op | source)
XLA Modules:
  0.0 74.4 jit_solution(11622643742427381451)
XLA Ops:
  0.6 3.1 %collective-permute-start = (f32[128,512]{1,0:T(8,128)}, f32[128,512]{1,0:T(8,128)S(1)}, u32[]{:S(2)}, u32[]{:S(2)}) collective-permute-start(f32[128,512]{1,0:T(8,128)} %bitcast.10), channel_id=1, source_target_pairs={{0,16},{8,24},{16,0},{24,8},{1,17},{9,25},{17,1},{25,9},{2,18},{10... | collective-permute-start | bytes 786440 | tf_op jit(solution)/shard_map/ppermute | solution.py:412
  3.7 6.5 %schur.1 = (bf16[512,1024]{1,0:T(8,128)(2,1)S(1)}, f32[2,1024]{1,0:T(2,128)S(1)}, f32[520,128]{1,0:T(8,128)S(1)}, f32[520,128]{1,0:T(8,128)S(1)}) custom-call(bf16[1024,1024]{1,0:T(8,128)(2,1)} %bitcast.8, bf16[1024,512]{1,0:T(8,128)(2,1)} %bitcast.13, f32[128,512]{1,0:T(8,128)} %bitcast.14, bf16[2,1024]{1,0:T(2,128)(2,1)} %bitcast.15, f32[2,128]{1,0:T(2,128)} %bitcast.16), custom_call_target="tpu_custom_call" | custom-call | tf_op jit(solution)/shard_map/schur/pallas_call | solution.py:451
  10.2 0.0 collective-permute-done.refs_2_
  10.3 0.1 collective-permute-start.1
  10.3 1.5 %collective-permute-done.1 = f32[520,128]{1,0:T(8,128)S(1)} collective-permute-done((f32[520,128]{1,0:T(8,128)S(1)}, f32[520,128]{1,0:T(8,128)S(1)}, u32[]{:S(2)}, u32[]{:S(2)}) %collective-permute-start.1) | collective-permute-done | bytes 266272 | tf_op jit(solution)/shard_map/ppermute | solution.py:412
  11.9 1.7 %collective-permute-start.2 = (f32[520,128]{1,0:T(8,128)S(1)}, f32[520,128]{1,0:T(8,128)S(1)}, u32[]{:S(2)}, u32[]{:S(2)}) collective-permute-start(f32[520,128]{1,0:T(8,128)S(1)} %add.15), channel_id=1, source_target_pairs={{0,16},{8,24},{16,0},{24,8},{1,17},{9,25},{17,1},{25,9},{2,18},{10... | collective-permute-start | bytes 798728 | tf_op jit(solution)/shard_map/ppermute | solution.py:412
  13.6 6.8 %collective-permute-done.2 = f32[520,128]{1,0:T(8,128)S(1)} collective-permute-done((f32[520,128]{1,0:T(8,128)S(1)}, f32[520,128]{1,0:T(8,128)S(1)}, u32[]{:S(2)}, u32[]{:S(2)}) %collective-permute-start.2) | collective-permute-done | bytes 266272 | tf_op jit(solution)/shard_map/ppermute | solution.py:412
  20.4 0.1 collective-permute-start.3
  20.5 0.5 collective-permute-start.4
  21.0 0.1 collective-permute-start.5
  21.1 1.3 %collective-permute-done.4.refs_1_ = f32[128,512]{1,0:T(8,128)S(1)} collective-permute-done((f32[128,512]{1,0:T(8,128)S(1)}, f32[128,512]{1,0:T(8,128)S(1)}, u32[]{:S(2)}, u32[]{:S(2)}) %collective-permute-start.4) | collective-permute-done | bytes 262176 | tf_op jit(solution)/shard_map/ppermute | solution.py:412
  22.4 0.4 collective-permute-done.5.refs_3_
  22.8 11.4 %node.1 = (f32[264,128]{1,0:T(8,128)S(1)}, f32[512,512]{1,0:T(8,128)S(1)}, f32[512,512]{1,0:T(8,128)S(1)}, f32[512,128]{1,0:T(8,128)S(1)}, f32[8,512]{1,0:T(8,128)S(1)}) custom-call(f32[520,128]{1,0:T(8,128)S(1)} %add.16.mine, f32[520,128]{1,0:T(8,128)S(1)} %collective-permute-done.3.other, f32[128,512]{1,0:T(8,128)S(1)} %bitcast.12, ...), custom_call_target="tpu_custom_call" | custom-call | tf_op jit(solution)/shard_map/node/pallas_call | solution.py:483
  34.2 1.7 %collective-permute-start.6 = (f32[264,128]{1,0:T(8,128)S(1)}, f32[264,128]{1,0:T(8,128)S(1)}, u32[]{:S(2)}, u32[]{:S(2)}) collective-permute-start(f32[264,128]{1,0:T(8,128)S(1)} %get-tuple-element.23), channel_id=1, source_target_pairs={{0,1},{1,0},{2,3},{3,2},{4,5},{5,4},{6,7},{7,6},{8,9},{9,8},{10,11... | collective-permute-start | bytes 405512 | tf_op jit(solution)/shard_map/ppermute | solution.py:412
  35.8 4.0 %collective-permute-done.6 = f32[264,128]{1,0:T(8,128)S(1)} collective-permute-done((f32[264,128]{1,0:T(8,128)S(1)}, f32[264,128]{1,0:T(8,128)S(1)}, u32[]{:S(2)}, u32[]{:S(2)}) %collective-permute-start.6) | collective-permute-done | bytes 135200 | tf_op jit(solution)/shard_map/ppermute | solution.py:412
  39.9 1.8 %collective-permute-start.7 = (f32[264,128]{1,0:T(8,128)S(1)}, f32[264,128]{1,0:T(8,128)S(1)}, u32[]{:S(2)}, u32[]{:S(2)}) collective-permute-start(f32[264,128]{1,0:T(8,128)S(1)} %add.17), channel_id=1, source_target_pairs={{0,2},{1,3},{2,0},{3,1},{4,6},{5,7},{6,4},{7,5},{8,10},{9,11},{10,... | collective-permute-start | bytes 405512 | tf_op jit(solution)/shard_map/ppermute | solution.py:412
  41.6 3.3 %collective-permute-done.7 = f32[264,128]{1,0:T(8,128)S(1)} collective-permute-done((f32[264,128]{1,0:T(8,128)S(1)}, f32[264,128]{1,0:T(8,128)S(1)}, u32[]{:S(2)}, u32[]{:S(2)}) %collective-permute-start.7) | collective-permute-done | bytes 135200 | tf_op jit(solution)/shard_map/ppermute | solution.py:412
  45.0 2.8 %collective-permute-start.8 = (f32[264,128]{1,0:T(8,128)S(1)}, f32[264,128]{1,0:T(8,128)S(1)}, u32[]{:S(2)}, u32[]{:S(2)}) collective-permute-start(f32[264,128]{1,0:T(8,128)S(1)} %add.18), channel_id=1, source_target_pairs={{0,4},{1,5},{2,6},{3,7},{4,0},{5,1},{6,2},{7,3},{8,12},{9,13},{10,... | collective-permute-start | bytes 405512 | tf_op jit(solution)/shard_map/ppermute | solution.py:412
  47.8 4.8 %collective-permute-done.8 = f32[264,128]{1,0:T(8,128)S(1)} collective-permute-done((f32[264,128]{1,0:T(8,128)S(1)}, f32[264,128]{1,0:T(8,128)S(1)}, u32[]{:S(2)}, u32[]{:S(2)}) %collective-permute-start.8) | collective-permute-done | bytes 135200 | tf_op jit(solution)/shard_map/ppermute | solution.py:412
  52.5 1.7 %collective-permute-start.10 = (f32[264,128]{1,0:T(8,128)S(1)}, f32[264,128]{1,0:T(8,128)S(1)}, u32[]{:S(2)}, u32[]{:S(2)}) collective-permute-start(f32[264,128]{1,0:T(8,128)S(1)} %add.19.refs_0_), channel_id=1, source_target_pairs={{0,16},{8,24},{16,0},{24,8},{1,17},{9,25},{17,1},{25,9},{2,18},{10... | collective-permute-start | bytes 405512 | tf_op jit(solution)/shard_map/ppermute | solution.py:412
  54.2 0.0 collective-permute-start.9
  54.2 3.4 %collective-permute-done.10.refs_2_ = f32[264,128]{1,0:T(8,128)S(1)} collective-permute-done((f32[264,128]{1,0:T(8,128)S(1)}, f32[264,128]{1,0:T(8,128)S(1)}, u32[]{:S(2)}, u32[]{:S(2)}) %collective-permute-start.10) | collective-permute-done | bytes 135200 | tf_op jit(solution)/shard_map/ppermute | solution.py:412
  57.6 1.3 %collective-permute-done.11.refs_3_ = f32[264,128]{1,0:T(8,128)S(1)} collective-permute-done((f32[264,128]{1,0:T(8,128)S(1)}, f32[264,128]{1,0:T(8,128)S(1)}, u32[]{:S(2)}, u32[]{:S(2)}) %collective-permute-start.11) | collective-permute-done | bytes 135200 | tf_op jit(solution)/shard_map/ppermute | solution.py:412
  59.0 15.2 %root.1 = (f32[2,1024]{1,0:T(2,128)}, f32[2,128]{1,0:T(2,128)}, f32[2,512]{1,0:T(2,128)}) custom-call(f32[264,128]{1,0:T(8,128)S(1)} %add.19.refs_0_, f32[264,128]{1,0:T(8,128)S(1)} %collective-permute-done.9.refs_1_, f32[264,128]{1,0:T(8,128)S(1)} %collective-permute-done.10.refs_2_, f32[264,128]{1,0:T(8,128)S(1)} %collective-permute-done.11.refs_3_, ...), custom_call_target="tpu_custom_call" | custom-call | tf_op jit(solution)/shard_map/root/pallas_call | solution.py:507
  (16 shorter events, 0.2 us)
Async XLA Ops:
  0.6 9.6 %collective-permute-start = (f32[128,512]{1,0:T(8,128)}, f32[128,512]{1,0:T(8,128)S(1)}, u32[]{:S(2)}, u32[]{:S(2)}) collective-permute-start(f32[128,512]{1,0:T(8,128)} %bitcast.10), channel_id=1, source_target_pairs={{0,16},{8,24},{16,0},{24,8},{1,17},{9,25},{17,1},{25,9},{2,18},{10... | collective-permute-start | bytes 786440 | tf_op jit(solution)/shard_map/ppermute | solution.py:412
  3.7 16.8 %copy-start.2 = (f32[1,128,512]{2,1,0:T(8,128)S(1)}, f32[1,128,512]{2,1,0:T(8,128)}, u32[]{:S(2)}) copy-start(f32[1,128,512]{2,1,0:T(8,128)} %param.13) | copy-start | bytes 786436
  10.3 1.6 %collective-permute-start.1 = (f32[520,128]{1,0:T(8,128)S(1)}, f32[520,128]{1,0:T(8,128)S(1)}, u32[]{:S(2)}, u32[]{:S(2)}) collective-permute-start(f32[520,128]{1,0:T(8,128)S(1)} %get-tuple-element.20), channel_id=1, source_target_pairs={{0,8},{8,0},{16,24},{24,16},{1,9},{9,1},{17,25},{25,17},{2,10},{10... | collective-permute-start | bytes 798728 | tf_op jit(solution)/shard_map/ppermute | solution.py:412
  11.9 47.1 %copy-start = (bf16[1,1,1024,1024]{3,2,1,0:T(8,128)(2,1)S(1)}, bf16[1,1,1024,1024]{3,2,1,0:T(8,128)(2,1)}, u32[]{:S(2)}) copy-start(bf16[1,1,1024,1024]{3,2,1,0:T(8,128)(2,1)} %param.8) | copy-start | bytes 6291460
  11.9 47.1 %copy-start.1 = (f32[512,512]{1,0:T(8,128)S(1)}, f32[512,512]{1,0:T(8,128)}, u32[]{:S(2)}) copy-start(f32[512,512]{1,0:T(8,128)} %refs_4_.1) | copy-start | bytes 3145732
  11.9 47.1 %copy-start.3 = (f32[2,512]{1,0:T(2,128)S(1)}, f32[2,512]{1,0:T(2,128)}, u32[]{:S(2)}) copy-start(f32[2,512]{1,0:T(2,128)} %refs_5_.1) | copy-start | bytes 12292
  11.9 8.5 %collective-permute-start.2 = (f32[520,128]{1,0:T(8,128)S(1)}, f32[520,128]{1,0:T(8,128)S(1)}, u32[]{:S(2)}, u32[]{:S(2)}) collective-permute-start(f32[520,128]{1,0:T(8,128)S(1)} %add.15), channel_id=1, source_target_pairs={{0,16},{8,24},{16,0},{24,8},{1,17},{9,25},{17,1},{25,9},{2,18},{10... | collective-permute-start | bytes 798728 | tf_op jit(solution)/shard_map/ppermute | solution.py:412
  20.4 2.4 %collective-permute-start.3 = (f32[520,128]{1,0:T(8,128)S(1)}, f32[520,128]{1,0:T(8,128)S(1)}, u32[]{:S(2)}, u32[]{:S(2)}) collective-permute-start(f32[520,128]{1,0:T(8,128)S(1)} %add.16.mine), channel_id=1, source_target_pairs={{0,8},{8,0},{16,24},{24,16},{1,9},{9,1},{17,25},{25,17},{2,10},{10... | collective-permute-start | bytes 798728 | tf_op jit(solution)/shard_map/ppermute | solution.py:412
  20.5 1.9 %collective-permute-start.4 = (f32[128,512]{1,0:T(8,128)S(1)}, f32[128,512]{1,0:T(8,128)S(1)}, u32[]{:S(2)}, u32[]{:S(2)}) collective-permute-start(f32[128,512]{1,0:T(8,128)S(1)} %bitcast.11), channel_id=1, source_target_pairs={{0,8},{8,0},{16,24},{24,16},{1,9},{9,1},{17,25},{25,17},{2,10},{10... | collective-permute-start | bytes 786440 | tf_op jit(solution)/shard_map/ppermute | solution.py:412
  21.0 1.8 %collective-permute-start.5 = (f32[128,512]{1,0:T(8,128)S(1)}, f32[128,512]{1,0:T(8,128)S(1)}, u32[]{:S(2)}, u32[]{:S(2)}) collective-permute-start(f32[128,512]{1,0:T(8,128)S(1)} %collective-permute-done.refs_2_), channel_id=1, source_target_pairs={{0,8},{8,0},{16,24},{24,16},{1,9},{9,1},{17,25},{25,17},{2,10},{10... | collective-permute-start | bytes 786440 | tf_op jit(solution)/shard_map/ppermute | solution.py:412
  34.2 5.7 %collective-permute-start.6 = (f32[264,128]{1,0:T(8,128)S(1)}, f32[264,128]{1,0:T(8,128)S(1)}, u32[]{:S(2)}, u32[]{:S(2)}) collective-permute-start(f32[264,128]{1,0:T(8,128)S(1)} %get-tuple-element.23), channel_id=1, source_target_pairs={{0,1},{1,0},{2,3},{3,2},{4,5},{5,4},{6,7},{7,6},{8,9},{9,8},{10,11... | collective-permute-start | bytes 405512 | tf_op jit(solution)/shard_map/ppermute | solution.py:412
  39.9 5.1 %collective-permute-start.7 = (f32[264,128]{1,0:T(8,128)S(1)}, f32[264,128]{1,0:T(8,128)S(1)}, u32[]{:S(2)}, u32[]{:S(2)}) collective-permute-start(f32[264,128]{1,0:T(8,128)S(1)} %add.17), channel_id=1, source_target_pairs={{0,2},{1,3},{2,0},{3,1},{4,6},{5,7},{6,4},{7,5},{8,10},{9,11},{10,... | collective-permute-start | bytes 405512 | tf_op jit(solution)/shard_map/ppermute | solution.py:412
  45.0 7.5 %collective-permute-start.8 = (f32[264,128]{1,0:T(8,128)S(1)}, f32[264,128]{1,0:T(8,128)S(1)}, u32[]{:S(2)}, u32[]{:S(2)}) collective-permute-start(f32[264,128]{1,0:T(8,128)S(1)} %add.18), channel_id=1, source_target_pairs={{0,4},{1,5},{2,6},{3,7},{4,0},{5,1},{6,2},{7,3},{8,12},{9,13},{10,... | collective-permute-start | bytes 405512 | tf_op jit(solution)/shard_map/ppermute | solution.py:412
  52.5 5.1 %collective-permute-start.10 = (f32[264,128]{1,0:T(8,128)S(1)}, f32[264,128]{1,0:T(8,128)S(1)}, u32[]{:S(2)}, u32[]{:S(2)}) collective-permute-start(f32[264,128]{1,0:T(8,128)S(1)} %add.19.refs_0_), channel_id=1, source_target_pairs={{0,16},{8,24},{16,0},{24,8},{1,17},{9,25},{17,1},{25,9},{2,18},{10... | collective-permute-start | bytes 405512 | tf_op jit(solution)/shard_map/ppermute | solution.py:412
  54.2 3.4 %collective-permute-start.9 = (f32[264,128]{1,0:T(8,128)S(1)}, f32[264,128]{1,0:T(8,128)S(1)}, u32[]{:S(2)}, u32[]{:S(2)}) collective-permute-start(f32[264,128]{1,0:T(8,128)S(1)} %add.19.refs_0_), channel_id=1, source_target_pairs={{0,8},{8,0},{16,24},{24,16},{1,9},{9,1},{17,25},{25,17},{2,10},{10... | collective-permute-start | bytes 405512 | tf_op jit(solution)/shard_map/ppermute | solution.py:412
  57.6 1.4 %collective-permute-start.11 = (f32[264,128]{1,0:T(8,128)S(1)}, f32[264,128]{1,0:T(8,128)S(1)}, u32[]{:S(2)}, u32[]{:S(2)}) collective-permute-start(f32[264,128]{1,0:T(8,128)S(1)} %collective-permute-done.10.refs_2_), channel_id=1, source_target_pairs={{0,8},{8,0},{16,24},{24,16},{1,9},{9,1},{17,25},{25,17},{2,10},{10... | collective-permute-start | bytes 405512 | tf_op jit(solution)/shard_map/ppermute | solution.py:412

commit v3 on v2

--- a/solution.py
+++ b/solution.py
@@ -4,6 +4,7 @@
 from jax.experimental import pallas as pl
 from jax.experimental.pallas import tpu as pltpu
 from jax.sharding import PartitionSpec as P
+
 
 F32, BF16 = jnp.float32, jnp.bfloat16
 NN, NT, TN = ((1,), (0,)), ((1,), (1,)), ((0,), (0,))
@@ -121,7 +122,7 @@
             self.work.pop(0)()
 
 
-def factorize(a, low, inv, queue, after):
+def factorize(a, low, inv, queue, after, known=0):
     size = a.shape[0] // PARTS
 
     def at(i, count=1):
@@ -131,12 +132,14 @@
         def store(g, value, k=k):
             inv[k * size + ROWS * g : k * size + ROWS * g + ROWS, :] = value
 
-        rows = [a[k * size + ROWS * g : k * size + ROWS * g + ROWS, at(k)] for g in range(size // ROWS)]
-        invert_factor(rows, store, queue.some)
-        queue.all()
+        if k >= known:
+            rows = [a[k * size + ROWS * g : k * size + ROWS * g + ROWS, at(k)] for g in range(size // ROWS)]
+            invert_factor(rows, store, queue.some)
+            queue.all()
         if k + 1 < PARTS:
-            block = exact(a[at(k + 1), at(k)], inv[at(k), :], NT)
-            low[at(k + 1), at(k)] = block
+            if k >= known:
+                low[at(k + 1), at(k)] = exact(a[at(k + 1), at(k)], inv[at(k), :], NT)
+            block = low[at(k + 1), at(k)]
             a[at(k + 1), at(k + 1)] = a[at(k + 1), at(k + 1)] - exact(block, block, NT)
         rest = PARTS - k - 2
         if rest > 0:
@@ -154,13 +157,8 @@
         after(k)
 
 
-def packed_blocks():
-    order = []
-    for j in range(PARTS):
-        if j % 2 == 0:
-            order.append(("pair", j))
-        order += [("block", i, j) for i in range(j + 1, PARTS)]
-    return order
+FIRST = (((0, 0),), ((1, 0),))
+REST = (((2, 0), (3, 0), (2, 1)), ((3, 1), (2, 2), (3, 2)))
 
 
 def lower_mask(size):
@@ -169,26 +167,25 @@
     return row, col
 
 
-def schur_kernel(factor_h, couple_h, diag_h, rights_h, rhs_h, rt, proj, keep, send, factor, couple, turned, diag, rights, rhs, full, pack, line, sems):
+def schur_kernel(factor_h, couple_h, diag_h, rights_h, rhs_h, rt, proj, keep_a, send_a, keep_b, send_b, factor, couple, diag, rights, rhs, full, first, rest, line, sems):
     me = lax.axis_index("scen")
     order, link = couple.shape
     share = diag.shape[0]
     size = link // PARTS
-    width = order // PARTS
-    loads = [pltpu.make_async_copy(couple_h, couple, sems.at[PARTS])]
+    width = order // 2
+    loads = [pltpu.make_async_copy(couple_h, couple, sems.at[0])]
     small = ((rights_h, rights), (diag_h, diag), (rhs_h, rhs))
-    small = [pltpu.make_async_copy(src, dst, sems.at[PARTS + 1 + n]) for n, (src, dst) in enumerate(small)]
-    for c in range(PARTS):
+    small = [pltpu.make_async_copy(src, dst, sems.at[3 + n]) for n, (src, dst) in enumerate(small)]
+    for c in range(2):
         cut = slice(c * width, (c + 1) * width)
-        loads.append(pltpu.make_async_copy(factor_h.at[:, cut], factor.at[:, cut], sems.at[c]))
+        loads.append(pltpu.make_async_copy(factor_h.at[:, cut], factor.at[:, cut], sems.at[1 + c]))
     for load in [*loads, *small]:
         load.start()
     loads[0].wait()
-    turned[...] = couple[...].T
-    for c in range(PARTS):
+    for c in range(2):
         cut = slice(c * width, (c + 1) * width)
         loads[1 + c].wait()
-        rt[:, cut] = dot(turned[...], factor[:, cut], NN).astype(BF16)
+        rt[:, cut] = dot(couple[...], factor[:, cut], TN).astype(BF16)
         if c == 0:
             small[0].wait()
         proj[:, cut] = dot(rights[...], factor[:, cut], NN)
@@ -211,31 +208,61 @@
         line[:, mine] = line[:, mine] + rhs[...]
         vec = line[...]
     row, col = lower_mask(size)
-    order = packed_blocks()
-    half = len(order) // 2
     spare = []
 
     def block(i, j):
         return full[i * size : (i + 1) * size, j * size : (j + 1) * size]
 
-    for n, entry in enumerate(order):
-        if entry[0] == "pair":
-            j = entry[1]
-            second = block(j + 1, j + 1)
-            value = jnp.where(row >= col, block(j, j), second)
-            spare.append(jnp.sum(jnp.where(row == col, second, 0.0), axis=0, keepdims=True))
-        else:
-            value = block(entry[1], entry[2])
-        pack[n // half, (n % half) * size : (n % half + 1) * size, :] = value
-    pack[0, half * size :, :] = jnp.concatenate([vec[:, j * size : (j + 1) * size] for j in range(PARTS)], 0)
+    core = lax.rem(me, 2)
+    for pack, halves in ((first, FIRST), (rest, REST)):
+        for h, entries in enumerate(halves):
+            for n, (i, j) in enumerate(entries):
+                value = block(i, j)
+                if i == j:
+                    second = block(j + 1, j + 1)
+                    value = jnp.where(row >= col, value, second)
+                    spare.append(jnp.sum(jnp.where(row == col, second, 0.0), axis=0, keepdims=True))
+                pack[h, n * size : (n + 1) * size, :] = value
+    tail = len(REST[0]) * size
+    rest[0, tail:, :] = jnp.concatenate([vec[:, j * size : (j + 1) * size] for j in range(PARTS)], 0)
     spare.append(jnp.zeros((2 * PARTS - len(spare), size), F32))
-    pack[1, half * size :, :] = jnp.concatenate(spare, 0)
-    core = lax.rem(me, 2)
-    keep[...] = pack[core]
-    send[...] = pack[1 - core]
-
-
-def node_kernel(mine, other, *refs):
+    rest[1, tail:, :] = jnp.concatenate(spare, 0)
+    for pack, keep, send in ((first, keep_a, send_a), (rest, keep_b, send_b)):
+        keep[...] = pack[core]
+        send[...] = pack[1 - core]
+
+
+def halves_of(mine, other, entries, size):
+    core = lax.rem(lax.axis_index("scen"), 2)
+
+    def read(h, r0, r1):
+        want = jnp.full((r1 - r0, size), h, jnp.int32) == core
+        return jnp.where(want, mine[r0:r1, :], other[r0:r1, :])
+
+    def block(i, j):
+        h = 0 if (i, j) in entries[0] else 1
+        n = entries[h].index((i, j))
+        return read(h, n * size, (n + 1) * size)
+
+    return read, block
+
+
+def head_kernel(mine, other, inv, under):
+    size = inv.shape[0]
+    _, block = halves_of(mine, other, FIRST, size)
+    row, col = lower_mask(size)
+    both = block(0, 0)
+    whole = jnp.where(row >= col, both, both.T)
+    rows = [whole[ROWS * g : ROWS * g + ROWS, :] for g in range(size // ROWS)]
+
+    def store(g, value):
+        inv[ROWS * g : ROWS * g + ROWS, :] = value
+
+    invert_factor(rows, store, lambda left: None)
+    under[...] = exact(block(1, 0), inv[...], NT)
+
+
+def node_kernel(mine_a, other_a, mine_b, other_b, inv_a, under, *refs):
     pieces, refs = refs[: refs_pieces(refs)], refs[refs_pieces(refs) :]
     strip, wide, low, inv, wz, a, link_full, acc, sems = refs
     me = lax.axis_index("scen")
@@ -246,37 +273,28 @@
         start = pl.multiple_of(lax.bitwise_xor(me, p) * share, ROWS)
         copies.append(pltpu.make_async_copy(piece, link_full.at[pl.ds(start, share), :], sems.at[p]))
         copies[-1].start()
-    core = lax.rem(me, 2)
-    order = packed_blocks()
-    half = len(order) // 2
     row, col = lower_mask(size)
-
-    def part(n, r0, r1):
-        want = jnp.full((r1 - r0, size), n // half, jnp.int32) == core
-        r0, r1 = (n % half) * size + r0, (n % half) * size + r1
-        return jnp.where(want, mine[r0:r1, :], other[r0:r1, :])
+    _, block_a = halves_of(mine_a, other_a, FIRST, size)
+    read_b, block_b = halves_of(mine_b, other_b, REST, size)
 
     def at(i, count=1):
         return slice(i * size, (i + count) * size)
 
-    vec = part(half - 1, size, size + 2 * PARTS)
-    spare = part(2 * half - 1, size, size + 2 * PARTS)
-    pairs = 0
-    for n, entry in enumerate(order):
-        if entry[0] == "pair":
-            j = entry[1]
-            both = part(n, 0, size)
-            flip = both.T
-            a[at(j), at(j)] = jnp.where(row >= col, both, flip)
-            edge = jnp.broadcast_to(spare[pairs : pairs + 1, :], (size, size))
-            a[at(j + 1), at(j + 1)] = jnp.where(row == col, edge, jnp.where(row < col, both, flip))
-            pairs += 1
-        else:
-            a[at(entry[1]), at(entry[2])] = part(n, 0, size)
+    tail = len(REST[0]) * size
+    vec, spare = read_b(0, tail, tail + 2 * PARTS), read_b(1, tail, tail + 2 * PARTS)
+    inv[at(0), :] = inv_a[...]
+    low[at(1), at(0)] = under[...]
+    for n, block in enumerate((block_a, block_b)):
+        both, edge = block(2 * n, 2 * n), jnp.broadcast_to(spare[n : n + 1, :], (size, size))
+        flip = both.T
+        if n > 0:
+            a[at(2 * n), at(2 * n)] = jnp.where(row >= col, both, flip)
+        a[at(2 * n + 1), at(2 * n + 1)] = jnp.where(row == col, edge, jnp.where(row < col, both, flip))
+    for i, j in (*REST[0], *REST[1]):
+        if i > j:
+            a[at(i), at(j)] = block_b(i, j)
     pad = jnp.zeros((ROWS - 2, size), F32)
     z = [jnp.concatenate([vec[2 * j : 2 * j + 2, :], pad], 0) for j in range(PARTS)]
-    for copy in copies:
-        copy.wait()
     queue = Queue()
     strip_of = lax.div(me * share, size)
     lanes = [pl.ds(pl.multiple_of(lax.rem(strip_of + PARTS - d, PARTS) * size, size), size) for d in range(3)]
@@ -284,6 +302,9 @@
 
     def after(k):
         def spread():
+            if k == 0:
+                for copy in copies:
+                    copy.wait()
             wide[at(k), :] = exact(inv[at(k), :], link_full[at(k), :], NN)
 
         def vector():
@@ -293,6 +314,7 @@
             def run():
                 term = exact(wide[at(k), lanes[0]], wide[at(k), lanes[d]], TN)
                 acc[at(d), :] = term if k == 0 else acc[at(d), :] + term
+
             return run
 
         def right():
@@ -308,7 +330,7 @@
         if k + 1 < PARTS:
             queue.add(coming)
 
-    factorize(a, low, inv, queue, after)
+    factorize(a, low, inv, queue, after, 1)
     queue.all()
     own, above, cross = acc[at(0), :], acc[at(1), :], acc[at(2), :]
     mixed = jnp.where(row >= col, own, cross)
@@ -330,18 +352,14 @@
 
 
 def root_kernel(*refs):
-    count = len(refs) - 26
+    count = len(refs) - 19
     pieces, refs = refs[:count], refs[count:]
-    root_diag, root_rhs, proj, wide_h, low_h, inv_h, wz_h, rt_h, factor_h, leaf, node, root = refs[:12]
-    wide, nlow, ninv, nwz, rt, factor, a, low, inv, strips, mixes, ends, whole, sems = refs[12:]
+    root_diag, root_rhs, proj, wide, nlow, ninv, nwz, rt, factor, leaf, node, root = refs[:12]
+    a, low, inv, strips, mixes, ends, whole = refs[12:]
     me = lax.axis_index("scen")
     link = root_diag.shape[0]
     size = link // PARTS
     share = (pieces[0].shape[0] - ROWS) // 2
-    copies = []
-    for n, (src, dst) in enumerate(((low_h, nlow), (inv_h, ninv), (wide_h, wide), (wz_h, nwz), (rt_h, rt), (factor_h, factor))):
-        copies.append(pltpu.make_async_copy(src, dst, sems.at[n]))
-        copies[-1].start()
 
     def at(i, count=1):
         return slice(i * size, (i + count) * size)
@@ -366,8 +384,6 @@
         a[at(i), at(i - 2)] = jnp.where(row == col, edge, jnp.where(row < col, mixes[at(i), :], flips[i - 2])) + root_diag[at(i), at(i - 2)]
     pad = jnp.zeros((ROWS - 2, size), F32)
     rhs = [jnp.concatenate([ends[ROWS * i : ROWS * i + 2, :] - root_rhs[:, at(i)], pad], 0) for i in range(PARTS)]
-    for copy in copies:
-        copy.wait()
     queue = Queue()
     u = {}
 
@@ -435,7 +451,7 @@
     anywhere = pl.BlockSpec(memory_space=pl.ANY)
     far = pl.BlockSpec(memory_space=pltpu.HBM)
 
-    def local(factors, couple, leaf_rhs, node_diag, node_rhs, link_root, root_diag, root_rhs):
+    def run(factors, couple, leaf_rhs, node_diag, node_rhs, link_root, root_diag, root_rhs):
         factor, coupling, rights = factors[0, 0], couple[0, 0], leaf_rhs[0, 0]
         order, link = coupling.shape
         share = node_diag.shape[1]
@@ -446,39 +462,63 @@
         rhs = node_rhs[0]
         if share % size:
             rhs = lax.dynamic_update_slice(jnp.zeros((2, link), F32), rhs, (0, me * share))
-        tall = PARTS * size + 2 * PARTS
-        flat = jax.ShapeDtypeStruct((tall, size), F32)
-        rt, projected, keep, send = pl.pallas_call(
+        tall = len(REST[0]) * size + 2 * PARTS
+        flat_a, flat_b = (jax.ShapeDtypeStruct((n, size), F32) for n in (size, tall))
+        rt, projected, keep_a, send_a, keep_b, send_b = pl.pallas_call(
             schur_kernel,
             out_shape=(
                 jax.ShapeDtypeStruct((link, order), BF16),
                 jax.ShapeDtypeStruct((2, order), F32),
-                flat,
-                flat,
+                flat_a,
+                flat_a,
+                flat_b,
+                flat_b,
             ),
             in_specs=[far] * 5,
-            out_specs=(vmem,) * 4,
+            out_specs=(vmem,) * 6,
             scratch_shapes=[
                 pltpu.VMEM((order, order), BF16),
                 pltpu.VMEM((order, link), BF16),
-                pltpu.VMEM((link, order), BF16),
                 pltpu.VMEM((share, link), F32),
                 pltpu.VMEM((2, order), BF16),
                 pltpu.VMEM(rhs.shape, F32),
                 pltpu.VMEM((link, link), F32),
+                pltpu.VMEM((2, size, size), F32),
                 pltpu.VMEM((2, tall, size), F32),
                 pltpu.VMEM((2, link), F32),
-                pltpu.SemaphoreType.DMA((PARTS + 4,)),
+                pltpu.SemaphoreType.DMA((6,)),
             ],
             name="schur",
             compiler_params=pltpu.CompilerParams(vmem_limit_bytes=GRANT),
         )(*[hbm(x) for x in (factor, coupling, node_diag[0], rights, rhs)])
-        send, links = lax.optimization_barrier((send, links))
+        mine_a = keep_a + swap(send_a, "scen", scen, 1)
+        mine_b = keep_b + swap(send_b, "scen", scen, 1)
+        mine_a, links = lax.optimization_barrier((mine_a, links))
+        back = []
+        if scen > 2:
+            for value in (mine_a, mine_b):
+                back.append(swap(value, "scen", scen, 2))
         links = spread(links, "scen", scen, down[-1:])
-        mine = keep + swap(send, "scen", scen, 1)
-        for bit in bits(scen, 2):
-            mine = mine + swap(mine, "scen", scen, bit)
-        other = swap(mine, "scen", scen, 1)
+        if back:
+            mine_a = mine_a + back[0]
+        for bit in bits(scen, 4):
+            mine_a = mine_a + swap(mine_a, "scen", scen, bit)
+        other_a = swap(mine_a, "scen", scen, 1)
+        corner = jax.ShapeDtypeStruct((size, size), F32)
+        inv_a, under = pl.pallas_call(
+            head_kernel,
+            out_shape=(corner, corner),
+            in_specs=[vmem, vmem],
+            out_specs=(vmem, vmem),
+            name="head",
+            compiler_params=pltpu.CompilerParams(vmem_limit_bytes=GRANT),
+        )(mine_a, other_a)
+        mine_b, inv_a = lax.optimization_barrier((mine_b, inv_a))
+        if back:
+            mine_b = mine_b + back[1]
+        for bit in bits(scen, 4):
+            mine_b = mine_b + swap(mine_b, "scen", scen, bit)
+        other_b = swap(mine_b, "scen", scen, 1)
         square = jax.ShapeDtypeStruct((link, link), F32)
         strip, wide, low, inv, wz = pl.pallas_call(
             node_kernel,
@@ -489,7 +529,7 @@
                 jax.ShapeDtypeStruct((link, size), F32),
                 jax.ShapeDtypeStruct((ROWS, link), F32),
             ),
-            in_specs=[vmem, vmem] + [anywhere] * scen,
+            in_specs=[vmem] * 6 + [anywhere] * scen,
             out_specs=(vmem,) * 5,
             scratch_shapes=[
                 pltpu.VMEM((link, link), F32),
@@ -499,7 +539,7 @@
             ],
             name="node",
             compiler_params=pltpu.CompilerParams(vmem_limit_bytes=GRANT),
-        )(mine, other, *[links[p] for p in range(scen)])
+        )(mine_a, other_a, mine_b, other_b, inv_a, under, *[links[p] for p in range(scen)])
         for bit in bits(node):
             strip = strip + swap(strip, "node", node, bit)
         strips = spread({0: strip}, "scen", scen, down)
@@ -511,15 +551,9 @@
                 jax.ShapeDtypeStruct((2, share if aligned else link), F32),
                 jax.ShapeDtypeStruct((2, link), F32),
             ),
-            in_specs=[vmem] * (scen + 3) + [anywhere] * 6,
+            in_specs=[vmem] * (scen + 9),
             out_specs=(vmem,) * 3,
             scratch_shapes=[
-                pltpu.VMEM((link, link), F32),
-                pltpu.VMEM((link, link), F32),
-                pltpu.VMEM((link, size), F32),
-                pltpu.VMEM((ROWS, link), F32),
-                pltpu.VMEM((link, order), BF16),
-                pltpu.VMEM((order, order), BF16),
                 pltpu.VMEM((link, link), F32),
                 pltpu.VMEM((link, link), F32),
                 pltpu.VMEM((link, size), F32),
@@ -527,7 +561,6 @@
                 pltpu.VMEM((link, size), F32),
                 pltpu.VMEM((PARTS * ROWS, size), F32),
                 pltpu.VMEM((ROWS, link), F32),
-                pltpu.SemaphoreType.DMA((6,)),
             ],
             name="root",
             compiler_params=pltpu.CompilerParams(vmem_limit_bytes=GRANT),
@@ -536,7 +569,7 @@
             solved = lax.dynamic_slice(solved, (0, me * share), (2, share))
         return (leaf[None, None], solved[None], root)
 
-    return local
+    return run
 
 
 def solution(mesh):

time: 74.5 us -> 75.6 us (1.015)
  starting transfers between devices: 13.3 us -> 15.6 us
  Pallas kernels: 33.1 us -> 31.1 us
  waiting for transfers between devices: 26.9 us -> 27.7 us
    ppermute x12 -> x15, starting transfers between devices: 13.3 us -> 15.6 us  [swap(): return lax.ppermute(x, axis, [(i, i ^ bit) for i in range(count)])]
    pallas_call x3 -> x4, Pallas kernels: 33.1 us -> 31.1 us  [the longest x1 14.8 us: run(): pl.pallas_call(root_kernel, out_shape=(jax.ShapeDtypeStruct((2, order), F...]
    ppermute x12 -> x15, waiting for transfers between devices: 26.9 us -> 27.7 us  [swap(): return lax.ppermute(x, axis, [(i, i ^ bit) for i in range(count)])]
  transfers between devices with their start and end apart: 12 -> 15, of which waited for: 9 -> 10; matrix products, arithmetic and copies ran while one was open for 0% -> 0% of each run, Pallas kernels for 9% -> 3%
where the time goes in v3:
time: 75.6 us; the launch traced here: 75.4 us
  Pallas kernels  31.1 us (41%)
  waiting for transfers between devices  27.7 us (37%)
  starting transfers between devices  15.6 us (21%)
    ppermute x15, waiting for transfers between devices, swap(): return lax.ppermute(x, axis, [(i, i ^ bit) for i in range(count)])  27.7 us
    ppermute x15, starting transfers between devices, swap(): return lax.ppermute(x, axis, [(i, i ^ bit) for i in range(count)])  15.6 us
    pallas_call x1, Pallas kernels, run(): pl.pallas_call(root_kernel, out_shape=(jax.ShapeDtypeStruct((2, order), F...  14.8 us
    pallas_call x1, Pallas kernels, run(): pl.pallas_call(node_kernel, out_shape=(jax.ShapeDtypeStruct((2 * share +...  9.34 us
    pallas_call x1, Pallas kernels, run(): pl.pallas_call(schur_kernel, out_shape=(jax.ShapeDtypeStruct((link, order...  4.64 us
    pallas_call x1, Pallas kernels, run(): pl.pallas_call(head_kernel, out_shape=(corner, corner), in_specs=[vmem, v...  2.41 us
  transfers between devices with their start and end apart: 15, of which 10 were waited for; matrix products, arithmetic and copies ran while one was open for 0% of the time, Pallas kernels for 3%

profile of v3, /device:TPU:0, one launch (start us, length us, event | category | flops | bytes accessed | tf_op | source)
XLA Modules:
  0.0 75.4 jit_solution(4060505034827559179)
XLA Ops:
  0.6 4.6 %schur.1 = (bf16[512,1024]{1,0:T(8,128)(2,1)S(1)}, f32[2,1024]{1,0:T(2,128)S(1)}, f32[128,128]{1,0:T(8,128)S(1)}, f32[128,128]{1,0:T(8,128)S(1)}, f32[392,128]{1,0:T(8,128)S(1)}, /*index=5*/f32[392,128]{1,0:T(8,128)S(1)}) custom-call(bf16[1024,1024]{1,0:T(8,128)(2,1)} %bitcast.8, bf16[1024,512]{1,0:T(8,128)(2,1)} %bitcast.13, f32[128,512]{1,0:T(8,128)} %bitcast.14, ...), custom_call_target="tpu_custom_call" | custom-call | tf_op jit(solution)/shard_map/schur/pallas_call | solution.py:467
  5.3 0.6 collective-permute-start.4
  5.8 2.6 %collective-permute-start.1 = (f32[128,512]{1,0:T(8,128)S(1)}, f32[128,512]{1,0:T(8,128)S(1)}, u32[]{:S(2)}, u32[]{:S(2)}) collective-permute-start(f32[128,512]{1,0:T(8,128)S(1)} %bitcast.10), channel_id=1, source_target_pairs={{0,16},{8,24},{16,0},{24,8},{1,17},{9,25},{17,1},{25,9},{2,18},{10... | collective-permute-start | bytes 786440 | tf_op jit(solution)/shard_map/ppermute | solution.py:428
  8.5 1.4 %collective-permute-start.5 = (f32[392,128]{1,0:T(8,128)S(1)}, f32[392,128]{1,0:T(8,128)S(1)}, u32[]{:S(2)}, u32[]{:S(2)}) collective-permute-start(f32[392,128]{1,0:T(8,128)S(1)} %add.23), channel_id=1, source_target_pairs={{0,16},{8,24},{16,0},{24,8},{1,17},{9,25},{17,1},{25,9},{2,18},{10... | collective-permute-start | bytes 602120 | tf_op jit(solution)/shard_map/ppermute | solution.py:428
  9.9 1.3 %collective-permute-done = f32[128,128]{1,0:T(8,128)S(1)} collective-permute-done((f32[128,128]{1,0:T(8,128)S(1)}, f32[128,128]{1,0:T(8,128)S(1)}, u32[]{:S(2)}, u32[]{:S(2)}) %collective-permute-start) | collective-permute-done | bytes 65568 | tf_op jit(solution)/shard_map/ppermute | solution.py:428
  11.2 4.4 %collective-permute-done.1.refs_2_ = f32[128,512]{1,0:T(8,128)S(1)} collective-permute-done((f32[128,512]{1,0:T(8,128)S(1)}, f32[128,512]{1,0:T(8,128)S(1)}, u32[]{:S(2)}, u32[]{:S(2)}) %collective-permute-start.1) | collective-permute-done | bytes 262176 | tf_op jit(solution)/shard_map/ppermute | solution.py:428
  15.6 2.0 %collective-permute-start.2 = (f32[128,128]{1,0:T(8,128)S(1)}, f32[128,128]{1,0:T(8,128)S(1)}, u32[]{:S(2)}, u32[]{:S(2)}) collective-permute-start(f32[128,128]{1,0:T(8,128)S(1)} %add.21), channel_id=1, source_target_pairs={{0,16},{8,24},{16,0},{24,8},{1,17},{9,25},{17,1},{25,9},{2,18},{10... | collective-permute-start | bytes 196616 | tf_op jit(solution)/shard_map/ppermute | solution.py:428
  17.6 3.4 %collective-permute-done.2 = f32[128,128]{1,0:T(8,128)S(1)} collective-permute-done((f32[128,128]{1,0:T(8,128)S(1)}, f32[128,128]{1,0:T(8,128)S(1)}, u32[]{:S(2)}, u32[]{:S(2)}) %collective-permute-start.2) | collective-permute-done | bytes 65568 | tf_op jit(solution)/shard_map/ppermute | solution.py:428
  21.1 0.5 collective-permute-start.7
  21.7 0.7 collective-permute-done.3.other.other_a
  22.4 2.4 %head.1 = (f32[128,128]{1,0:T(8,128)S(1)}, f32[128,128]{1,0:T(8,128)S(1)}) custom-call(f32[128,128]{1,0:T(8,128)S(1)} %add.22.mine.mine_a, f32[128,128]{1,0:T(8,128)S(1)} %collective-permute-done.3.other.other_a), custom_call_target="tpu_custom_call" | custom-call | tf_op jit(solution)/shard_map/head/pallas_call | solution.py:508
  24.8 0.2 collective-permute-start.6
  25.1 1.3 %collective-permute-done.6.other_b = f32[392,128]{1,0:T(8,128)S(1)} collective-permute-done((f32[392,128]{1,0:T(8,128)S(1)}, f32[392,128]{1,0:T(8,128)S(1)}, u32[]{:S(2)}, u32[]{:S(2)}) %collective-permute-start.6) | collective-permute-done | bytes 200736 | tf_op jit(solution)/shard_map/ppermute | solution.py:428
  26.3 9.3 %node.1 = (f32[264,128]{1,0:T(8,128)S(1)}, f32[512,512]{1,0:T(8,128)S(1)}, f32[512,512]{1,0:T(8,128)S(1)}, f32[512,128]{1,0:T(8,128)S(1)}, f32[8,512]{1,0:T(8,128)S(1)}) custom-call(f32[128,128]{1,0:T(8,128)S(1)} %add.22.mine.mine_a, f32[128,128]{1,0:T(8,128)S(1)} %collective-permute-done.3.other.other_a, f32[392,128]{1,0:T(8,128)S(1)} %add.24.mine_b, ...), custom_call_target="tpu_custom_call" | custom-call | tf_op jit(solution)/shard_map/node/pallas_call | solution.py:523
  35.7 1.8 %collective-permute-start.9 = (f32[264,128]{1,0:T(8,128)S(1)}, f32[264,128]{1,0:T(8,128)S(1)}, u32[]{:S(2)}, u32[]{:S(2)}) collective-permute-start(f32[264,128]{1,0:T(8,128)S(1)} %get-tuple-element.35), channel_id=1, source_target_pairs={{0,1},{1,0},{2,3},{3,2},{4,5},{5,4},{6,7},{7,6},{8,9},{9,8},{10,11... | collective-permute-start | bytes 405512 | tf_op jit(solution)/shard_map/ppermute | solution.py:428
  37.5 3.9 %collective-permute-done.9 = f32[264,128]{1,0:T(8,128)S(1)} collective-permute-done((f32[264,128]{1,0:T(8,128)S(1)}, f32[264,128]{1,0:T(8,128)S(1)}, u32[]{:S(2)}, u32[]{:S(2)}) %collective-permute-start.9) | collective-permute-done | bytes 135200 | tf_op jit(solution)/shard_map/ppermute | solution.py:428
  41.4 1.9 %collective-permute-start.10 = (f32[264,128]{1,0:T(8,128)S(1)}, f32[264,128]{1,0:T(8,128)S(1)}, u32[]{:S(2)}, u32[]{:S(2)}) collective-permute-start(f32[264,128]{1,0:T(8,128)S(1)} %add.25), channel_id=1, source_target_pairs={{0,2},{1,3},{2,0},{3,1},{4,6},{5,7},{6,4},{7,5},{8,10},{9,11},{10,... | collective-permute-start | bytes 405512 | tf_op jit(solution)/shard_map/ppermute | solution.py:428
  43.3 3.2 %collective-permute-done.10 = f32[264,128]{1,0:T(8,128)S(1)} collective-permute-done((f32[264,128]{1,0:T(8,128)S(1)}, f32[264,128]{1,0:T(8,128)S(1)}, u32[]{:S(2)}, u32[]{:S(2)}) %collective-permute-start.10) | collective-permute-done | bytes 135200 | tf_op jit(solution)/shard_map/ppermute | solution.py:428
  46.5 2.9 %collective-permute-start.11 = (f32[264,128]{1,0:T(8,128)S(1)}, f32[264,128]{1,0:T(8,128)S(1)}, u32[]{:S(2)}, u32[]{:S(2)}) collective-permute-start(f32[264,128]{1,0:T(8,128)S(1)} %add.26), channel_id=1, source_target_pairs={{0,4},{1,5},{2,6},{3,7},{4,0},{5,1},{6,2},{7,3},{8,12},{9,13},{10,... | collective-permute-start | bytes 405512 | tf_op jit(solution)/shard_map/ppermute | solution.py:428
  49.4 4.8 %collective-permute-done.11 = f32[264,128]{1,0:T(8,128)S(1)} collective-permute-done((f32[264,128]{1,0:T(8,128)S(1)}, f32[264,128]{1,0:T(8,128)S(1)}, u32[]{:S(2)}, u32[]{:S(2)}) %collective-permute-start.11) | collective-permute-done | bytes 135200 | tf_op jit(solution)/shard_map/ppermute | solution.py:428
  54.2 1.6 %collective-permute-start.13 = (f32[264,128]{1,0:T(8,128)S(1)}, f32[264,128]{1,0:T(8,128)S(1)}, u32[]{:S(2)}, u32[]{:S(2)}) collective-permute-start(f32[264,128]{1,0:T(8,128)S(1)} %add.27.refs_0_), channel_id=1, source_target_pairs={{0,16},{8,24},{16,0},{24,8},{1,17},{9,25},{17,1},{25,9},{2,18},{10... | collective-permute-start | bytes 405512 | tf_op jit(solution)/shard_map/ppermute | solution.py:428
  55.9 3.4 %collective-permute-done.13.refs_2_ = f32[264,128]{1,0:T(8,128)S(1)} collective-permute-done((f32[264,128]{1,0:T(8,128)S(1)}, f32[264,128]{1,0:T(8,128)S(1)}, u32[]{:S(2)}, u32[]{:S(2)}) %collective-permute-start.13) | collective-permute-done | bytes 135200 | tf_op jit(solution)/shard_map/ppermute | solution.py:428
  59.3 1.3 %collective-permute-done.14.refs_3_ = f32[264,128]{1,0:T(8,128)S(1)} collective-permute-done((f32[264,128]{1,0:T(8,128)S(1)}, f32[264,128]{1,0:T(8,128)S(1)}, u32[]{:S(2)}, u32[]{:S(2)}) %collective-permute-start.14) | collective-permute-done | bytes 135200 | tf_op jit(solution)/shard_map/ppermute | solution.py:428
  60.6 14.8 %root.1 = (f32[2,1024]{1,0:T(2,128)}, f32[2,128]{1,0:T(2,128)}, f32[2,512]{1,0:T(2,128)}) custom-call(f32[264,128]{1,0:T(8,128)S(1)} %add.27.refs_0_, f32[264,128]{1,0:T(8,128)S(1)} %collective-permute-done.12.refs_1_, f32[264,128]{1,0:T(8,128)S(1)} %collective-permute-done.13.refs_2_, f32[264,128]{1,0:T(8,128)S(1)} %collective-permute-done.14.refs_3_, ...), custom_call_target="tpu_custom_call" | custom-call | tf_op jit(solution)/shard_map/root/pallas_call | solution.py:547
  (25 shorter events, 0.3 us)
Async XLA Ops:
  0.6 5.2 %copy-start.2 = (f32[1,128,512]{2,1,0:T(8,128)S(1)}, f32[1,128,512]{2,1,0:T(8,128)}, u32[]{:S(2)}) copy-start(f32[1,128,512]{2,1,0:T(8,128)} %param.13) | copy-start | bytes 786436
  5.3 3.1 %collective-permute-start.4 = (f32[392,128]{1,0:T(8,128)S(1)}, f32[392,128]{1,0:T(8,128)S(1)}, u32[]{:S(2)}, u32[]{:S(2)}) collective-permute-start(f32[392,128]{1,0:T(8,128)S(1)} %get-tuple-element.28), channel_id=1, source_target_pairs={{0,8},{8,0},{16,24},{24,16},{1,9},{9,1},{17,25},{25,17},{2,10},{10... | collective-permute-start | bytes 602120 | tf_op jit(solution)/shard_map/ppermute | solution.py:428
  5.8 9.7 %collective-permute-start.1 = (f32[128,512]{1,0:T(8,128)S(1)}, f32[128,512]{1,0:T(8,128)S(1)}, u32[]{:S(2)}, u32[]{:S(2)}) collective-permute-start(f32[128,512]{1,0:T(8,128)S(1)} %bitcast.10), channel_id=1, source_target_pairs={{0,16},{8,24},{16,0},{24,8},{1,17},{9,25},{17,1},{25,9},{2,18},{10... | collective-permute-start | bytes 786440 | tf_op jit(solution)/shard_map/ppermute | solution.py:428
  8.5 52.2 %copy-start = (bf16[1,1,1024,1024]{3,2,1,0:T(8,128)(2,1)S(1)}, bf16[1,1,1024,1024]{3,2,1,0:T(8,128)(2,1)}, u32[]{:S(2)}) copy-start(bf16[1,1,1024,1024]{3,2,1,0:T(8,128)(2,1)} %param.8) | copy-start | bytes 6291460
  8.5 52.2 %copy-start.1 = (f32[512,512]{1,0:T(8,128)S(1)}, f32[512,512]{1,0:T(8,128)}, u32[]{:S(2)}) copy-start(f32[512,512]{1,0:T(8,128)} %refs_4_.1) | copy-start | bytes 3145732
  8.5 52.2 %copy-start.3 = (f32[2,512]{1,0:T(2,128)S(1)}, f32[2,512]{1,0:T(2,128)}, u32[]{:S(2)}) copy-start(f32[2,512]{1,0:T(2,128)} %refs_5_.1) | copy-start | bytes 12292
  8.5 16.3 %collective-permute-start.5 = (f32[392,128]{1,0:T(8,128)S(1)}, f32[392,128]{1,0:T(8,128)S(1)}, u32[]{:S(2)}, u32[]{:S(2)}) collective-permute-start(f32[392,128]{1,0:T(8,128)S(1)} %add.23), channel_id=1, source_target_pairs={{0,16},{8,24},{16,0},{24,8},{1,17},{9,25},{17,1},{25,9},{2,18},{10... | collective-permute-start | bytes 602120 | tf_op jit(solution)/shard_map/ppermute | solution.py:428
  9.9 1.3 %collective-permute-start = (f32[128,128]{1,0:T(8,128)S(1)}, f32[128,128]{1,0:T(8,128)S(1)}, u32[]{:S(2)}, u32[]{:S(2)}) collective-permute-start(f32[128,128]{1,0:T(8,128)S(1)} %get-tuple-element.25), channel_id=1, source_target_pairs={{0,8},{8,0},{16,24},{24,16},{1,9},{9,1},{17,25},{25,17},{2,10},{10... | collective-permute-start | bytes 196616 | tf_op jit(solution)/shard_map/ppermute | solution.py:428
  15.6 5.4 %collective-permute-start.2 = (f32[128,128]{1,0:T(8,128)S(1)}, f32[128,128]{1,0:T(8,128)S(1)}, u32[]{:S(2)}, u32[]{:S(2)}) collective-permute-start(f32[128,128]{1,0:T(8,128)S(1)} %add.21), channel_id=1, source_target_pairs={{0,16},{8,24},{16,0},{24,8},{1,17},{9,25},{17,1},{25,9},{2,18},{10... | collective-permute-start | bytes 196616 | tf_op jit(solution)/shard_map/ppermute | solution.py:428
  21.0 1.3 %collective-permute-start.3 = (f32[128,128]{1,0:T(8,128)S(1)}, f32[128,128]{1,0:T(8,128)S(1)}, u32[]{:S(2)}, u32[]{:S(2)}) collective-permute-start(f32[128,128]{1,0:T(8,128)S(1)} %add.22.mine.mine_a), channel_id=1, source_target_pairs={{0,8},{8,0},{16,24},{24,16},{1,9},{9,1},{17,25},{25,17},{2,10},{10... | collective-permute-start | bytes 196616 | tf_op jit(solution)/shard_map/ppermute | solution.py:428
  21.1 3.9 %collective-permute-start.7 = (f32[128,512]{1,0:T(8,128)S(1)}, f32[128,512]{1,0:T(8,128)S(1)}, u32[]{:S(2)}, u32[]{:S(2)}) collective-permute-start(f32[128,512]{1,0:T(8,128)S(1)} %bitcast.11), channel_id=1, source_target_pairs={{0,8},{8,0},{16,24},{24,16},{1,9},{9,1},{17,25},{25,17},{2,10},{10... | collective-permute-start | bytes 786440 | tf_op jit(solution)/shard_map/ppermute | solution.py:428
  21.6 3.4 %collective-permute-start.8 = (f32[128,512]{1,0:T(8,128)S(1)}, f32[128,512]{1,0:T(8,128)S(1)}, u32[]{:S(2)}, u32[]{:S(2)}) collective-permute-start(f32[128,512]{1,0:T(8,128)S(1)} %collective-permute-done.1.refs_2_), channel_id=1, source_target_pairs={{0,8},{8,0},{16,24},{24,16},{1,9},{9,1},{17,25},{25,17},{2,10},{10... | collective-permute-start | bytes 786440 | tf_op jit(solution)/shard_map/ppermute | solution.py:428
  24.8 1.5 %collective-permute-start.6 = (f32[392,128]{1,0:T(8,128)S(1)}, f32[392,128]{1,0:T(8,128)S(1)}, u32[]{:S(2)}, u32[]{:S(2)}) collective-permute-start(f32[392,128]{1,0:T(8,128)S(1)} %add.24.mine_b), channel_id=1, source_target_pairs={{0,8},{8,0},{16,24},{24,16},{1,9},{9,1},{17,25},{25,17},{2,10},{10... | collective-permute-start | bytes 602120 | tf_op jit(solution)/shard_map/ppermute | solution.py:428
  35.7 5.7 %collective-permute-start.9 = (f32[264,128]{1,0:T(8,128)S(1)}, f32[264,128]{1,0:T(8,128)S(1)}, u32[]{:S(2)}, u32[]{:S(2)}) collective-permute-start(f32[264,128]{1,0:T(8,128)S(1)} %get-tuple-element.35), channel_id=1, source_target_pairs={{0,1},{1,0},{2,3},{3,2},{4,5},{5,4},{6,7},{7,6},{8,9},{9,8},{10,11... | collective-permute-start | bytes 405512 | tf_op jit(solution)/shard_map/ppermute | solution.py:428
  41.4 5.1 %collective-permute-start.10 = (f32[264,128]{1,0:T(8,128)S(1)}, f32[264,128]{1,0:T(8,128)S(1)}, u32[]{:S(2)}, u32[]{:S(2)}) collective-permute-start(f32[264,128]{1,0:T(8,128)S(1)} %add.25), channel_id=1, source_target_pairs={{0,2},{1,3},{2,0},{3,1},{4,6},{5,7},{6,4},{7,5},{8,10},{9,11},{10,... | collective-permute-start | bytes 405512 | tf_op jit(solution)/shard_map/ppermute | solution.py:428
  46.5 7.7 %collective-permute-start.11 = (f32[264,128]{1,0:T(8,128)S(1)}, f32[264,128]{1,0:T(8,128)S(1)}, u32[]{:S(2)}, u32[]{:S(2)}) collective-permute-start(f32[264,128]{1,0:T(8,128)S(1)} %add.26), channel_id=1, source_target_pairs={{0,4},{1,5},{2,6},{3,7},{4,0},{5,1},{6,2},{7,3},{8,12},{9,13},{10,... | collective-permute-start | bytes 405512 | tf_op jit(solution)/shard_map/ppermute | solution.py:428
  54.2 5.1 %collective-permute-start.13 = (f32[264,128]{1,0:T(8,128)S(1)}, f32[264,128]{1,0:T(8,128)S(1)}, u32[]{:S(2)}, u32[]{:S(2)}) collective-permute-start(f32[264,128]{1,0:T(8,128)S(1)} %add.27.refs_0_), channel_id=1, source_target_pairs={{0,16},{8,24},{16,0},{24,8},{1,17},{9,25},{17,1},{25,9},{2,18},{10... | collective-permute-start | bytes 405512 | tf_op jit(solution)/shard_map/ppermute | solution.py:428
  55.8 3.4 %collective-permute-start.12 = (f32[264,128]{1,0:T(8,128)S(1)}, f32[264,128]{1,0:T(8,128)S(1)}, u32[]{:S(2)}, u32[]{:S(2)}) collective-permute-start(f32[264,128]{1,0:T(8,128)S(1)} %add.27.refs_0_), channel_id=1, source_target_pairs={{0,8},{8,0},{16,24},{24,16},{1,9},{9,1},{17,25},{25,17},{2,10},{10... | collective-permute-start | bytes 405512 | tf_op jit(solution)/shard_map/ppermute | solution.py:428
  59.3 1.4 %collective-permute-start.14 = (f32[264,128]{1,0:T(8,128)S(1)}, f32[264,128]{1,0:T(8,128)S(1)}, u32[]{:S(2)}, u32[]{:S(2)}) collective-permute-start(f32[264,128]{1,0:T(8,128)S(1)} %collective-permute-done.13.refs_2_), channel_id=1, source_target_pairs={{0,8},{8,0},{16,24},{24,16},{1,9},{9,1},{17,25},{25,17},{2,10},{10... | collective-permute-start | bytes 405512 | tf_op jit(solution)/shard_map/ppermute | solution.py:428
